TPU v7x, 512 devices: a whole 4x4x16 slice. The times are simulated.
512 devices in a mesh: ctx: 32 (over y, x, core), ch: 16 (over z).
Axes of the slice: x: 4, y: 4, z: 16, core: 2. Of those that a mesh axis runs over, the one named last changes fastest.
Arguments:
- stream: bfloat16 [16384, 4096], P('ctx', 'ch'), may hold values from -900 to 900
- key_gate: bfloat16 [16384, 4096], P('ctx', 'ch'), may hold values from -6 to 6
- query_gate: bfloat16 [16384, 4096], P('ctx', 'ch'), may hold values from -6 to 6
- grad_output: bfloat16 [16384, 4096], P('ctx', 'ch'), may hold values from -50 to 50
- norm_gain: float32 [4096], P('ch'), may hold values from 0.1 to 1.9
- residue: float32 [4096, 16], P('ch'), may hold values from -0.5 to 0.5
- log_rate: float32 [4096, 16], P('ch'), may hold values from -14 to -2.9
Outputs:
- output: bfloat16 [16384, 4096], P('ctx', 'ch')
- grad_stream: bfloat16 [16384, 4096], P('ctx', 'ch')
- grad_key: bfloat16 [16384, 4096], P('ctx', 'ch')
- grad_query: bfloat16 [16384, 4096], P('ctx', 'ch')
- grad_gain: float32 [4096], P('ch')
- grad_residue: float32 [4096, 16], P('ch')
- grad_rate: float32 [4096, 16], P('ch')
All inputs are finite; a program needn't handle non-finite values.
Results may differ from a plain program's by a relative error of at most 0.008.
Values sent between devices are 32-bit elements; how exact they have to be, the bound alone decides.
No kernel may reach another device: no remote copies, remote signals or barrier semaphores. Data moves between devices by JAX's collectives and lax.ppermute only.
A program may use at most 128 MiB of HBM per device.

v0:
```python
import math

import jax
import jax.numpy as jnp
from jax import lax
from jax.sharding import PartitionSpec as P

D = 4096


epsilon = 1e-05
block_rows = 128
highest = lax.Precision.HIGHEST


def toeplitz(residue, decay_rate, block_len):
    lags = jnp.arange(block_len, dtype=jnp.float32)
    falling = residue[:, :, None] * jnp.exp(-decay_rate[:, :, None] * lags)
    rising = jnp.exp(decay_rate[:, :, None] * lags)
    full = jnp.einsum("cmi,cmj->cij", falling, rising, precision=highest)
    rows = lax.broadcasted_iota(jnp.int32, (block_len, block_len), 0)
    cols = lax.broadcasted_iota(jnp.int32, (block_len, block_len), 1)
    return jnp.where((rows >= cols)[None, :, :], full, 0.0)


def lag_powers(decay_rate, block_len):
    lags = jnp.arange(block_len, dtype=jnp.float32)
    return jnp.exp(-decay_rate[:, :, None] * lags)


def chain_step(earlier, latter):
    return (earlier[0] * latter[0], latter[0] * earlier[1] + latter[1])


def local_zero(signal, residue, log_rate):
    decay_rate = jnp.exp(log_rate)
    channels, length = signal.shape
    block_len = min(block_rows, length)
    block_count = length // block_len
    powers = lag_powers(decay_rate, block_len)
    blocks = signal.reshape(channels, block_count, block_len)
    within = jnp.einsum(
        "cij,cnj->cni", toeplitz(residue, decay_rate, block_len), blocks, precision=highest
    )
    contrib = jnp.einsum("cnj,cmj->cnm", blocks, powers[:, :, ::-1], precision=highest)
    factor = jnp.broadcast_to(jnp.exp(-decay_rate * block_len)[:, None, :], contrib.shape)
    _, states = lax.associative_scan(chain_step, (factor, contrib), axis=1)
    before = jnp.concatenate([jnp.zeros_like(states[:, :1]), states[:, :-1]], axis=1)
    leading = residue[:, :, None] * powers * jnp.exp(-decay_rate)[:, :, None]
    across = jnp.einsum("cnm,cmi->cni", before, leading, precision=highest)
    return ((within + across).reshape(channels, length), states[:, -1])


def local(stream, key_gate, query_gate, grad_output, norm_gain, residue, log_rate):
    row_count, channels = stream.shape
    wide_stream = stream.astype(jnp.float32)
    square_sum = lax.psum(jnp.sum(wide_stream * wide_stream, axis=1), "ch")
    inv_rms = lax.rsqrt(square_sum / D + epsilon)[:, None]
    unit_stream = wide_stream * inv_rms
    normed = unit_stream * norm_gain
    key_wide = key_gate.astype(jnp.float32)
    query_wide = query_gate.astype(jnp.float32)
    grad_wide = grad_output.astype(jnp.float32)
    signal = (key_wide * normed).astype(jnp.bfloat16)
    grad_conv = grad_wide * query_wide
    signal_cols = signal.T.astype(jnp.float32)
    grad_cols = grad_conv.T
    moved = (
        lax.all_to_all(signal_cols, "ctx", split_axis=0, concat_axis=1, tiled=True),
        lax.all_to_all(grad_cols, "ctx", split_axis=0, concat_axis=1, tiled=True),
    )
    width = channels // lax.axis_size("ctx")
    first = lax.axis_index("ctx") * width
    residue_part = lax.dynamic_slice_in_dim(residue, first, width, 0)
    rate_part = lax.dynamic_slice_in_dim(log_rate, first, width, 0)
    (conv_part, unused_state), pullback = jax.vjp(local_zero, moved[0], residue_part, rate_part)
    grad_part, residue_piece, rate_piece = pullback((moved[1], jnp.zeros_like(residue_part)))
    conv_cols, grad_signal = (
        lax.all_to_all(conv_part, "ctx", split_axis=1, concat_axis=0, tiled=True),
        lax.all_to_all(grad_part, "ctx", split_axis=1, concat_axis=0, tiled=True),
    )
    residue_term = lax.dynamic_update_slice_in_dim(jnp.zeros_like(residue), residue_piece, first, 0)
    rate_term = lax.dynamic_update_slice_in_dim(jnp.zeros_like(log_rate), rate_piece, first, 0)
    conv_rows = conv_cols.T
    grad_rows = grad_signal.T
    output = (query_wide * conv_rows).astype(jnp.bfloat16)
    grad_query = (grad_wide * conv_rows).astype(jnp.bfloat16)
    grad_key = (grad_rows * normed).astype(jnp.bfloat16)
    grad_normed = grad_rows * key_wide
    gain_term = jnp.sum(grad_normed * unit_stream, axis=0)
    grad_unit = grad_normed * norm_gain
    inner_sum = lax.psum(jnp.sum(grad_unit * unit_stream, axis=1), "ch")
    grad_stream = (inv_rms * (grad_unit - unit_stream * (inner_sum / D)[:, None])).astype(
        jnp.bfloat16
    )
    scale = 1.0 / math.sqrt(row_count * lax.axis_size("ctx"))
    grad_residue, grad_rate, grad_gain = lax.psum((residue_term, rate_term, gain_term), "ctx")
    return (
        output,
        grad_stream,
        grad_key,
        grad_query,
        grad_gain * scale,
        grad_residue * scale,
        grad_rate * scale,
    )


def solution(mesh):
    placed = (
        P("ctx", "ch"),
        P("ctx", "ch"),
        P("ctx", "ch"),
        P("ctx", "ch"),
        P("ch"),
        P("ch", None),
        P("ch", None),
    )
    return jax.shard_map(
        local,
        mesh=mesh,
        in_specs=placed,
        out_specs=(
            P("ctx", "ch"),
            P("ctx", "ch"),
            P("ctx", "ch"),
            P("ctx", "ch"),
            P("ch"),
            P("ch", None),
            P("ch", None),
        ),
        check_vma=False,
    )
```

profile of v0, /device:TPU:32, one launch (start us, length us, event | category | flops | bytes accessed | tf_op | source)
XLA Modules:
  0.0 383.3 jit_solution(14185563819151338465)
XLA Ops:
  1.8 34.4 %psum.35 = f32[512]{0:T(512)S(1)} all-reduce(f32[512]{0:T(512)S(1)} %fusion.15), channel_id=1, replica_groups=mesh['ctx'=32,'ch'=16] {'ch'}, use_global_device_ids=true, to_apply=%region_1.0 | all-reduce | flops 512 | bytes 4096 | tf_op jit(solution)/shard_map/psum | solution.py:57
  37.8 7.5 %all-to-all-start = ((f32[32,8,512]{2,1,0:T(8,128)}), f32[32,8,512]{2,1,0:T(8,128)S(1)}, u32[]{:S(2)}, u32[]{:S(2)}) async-start(f32[32,8,512]{2,1,0:T(8,128)} %convert_bitcast_fusion), calls=%async_computation | async-start | bytes 1048576 | tf_op jit(solution)/shard_map/all_to_all | solution.py:69
  47.8 9.1 %all-to-all-done = f32[32,8,512]{2,1,0:T(8,128)S(1)} async-done(((f32[32,8,512]{2,1,0:T(8,128)}), f32[32,8,512]{2,1,0:T(8,128)S(1)}, u32[]{:S(2)}, u32[]{:S(2)}) %all-to-all-start) | async-done | bytes 524320 | tf_op jit(solution)/shard_map/all_to_all | solution.py:69
  77.4 1.6 pad.418
  79.1 1.6 pad.353
  83.7 4.0 %all-to-all-start.1 = ((f32[8,32,512]{2,0,1:T(8,128)}), f32[8,32,512]{2,0,1:T(8,128)S(1)}, u32[]{:S(2)}, u32[]{:S(2)}) async-start(f32[8,32,512]{2,0,1:T(8,128)} %copy.81), calls=%async_computation.1 | async-start | bytes 1048576 | tf_op jit(solution)/shard_map/all_to_all | solution.py:79
  89.6 9.8 %all-to-all-done.1 = f32[8,32,512]{2,0,1:T(8,128)S(1)} async-done(((f32[8,32,512]{2,0,1:T(8,128)}), f32[8,32,512]{2,0,1:T(8,128)S(1)}, u32[]{:S(2)}, u32[]{:S(2)}) %all-to-all-start.1) | async-done | bytes 524320 | tf_op jit(solution)/shard_map/all_to_all | solution.py:79
  99.3 2.0 fusion.17
  101.3 4.1 %all-to-all-start.2 = ((f32[32,8,512]{2,1,0:T(8,128)}), f32[32,8,512]{2,1,0:T(8,128)S(1)}, u32[]{:S(2)}, u32[]{:S(2)}) async-start(f32[32,8,512]{2,1,0:T(8,128)} %get-tuple-element.62), calls=%async_computation.2 | async-start | bytes 1048576 | tf_op jit(solution)/shard_map/all_to_all | solution.py:70
  107.1 9.7 %all-to-all-done.2 = f32[32,8,512]{2,1,0:T(8,128)S(1)} async-done(((f32[32,8,512]{2,1,0:T(8,128)}), f32[32,8,512]{2,1,0:T(8,128)S(1)}, u32[]{:S(2)}, u32[]{:S(2)}) %all-to-all-start.2) | async-done | bytes 524320 | tf_op jit(solution)/shard_map/all_to_all | solution.py:70
  117.1 1.7 fusion.18
  118.8 1.8 slice.239
  123.1 2.6 slice.240
  146.1 3.4 pad.307
  149.5 3.4 pad.308
  152.8 3.3 pad.326
  156.2 3.4 pad.327
  160.2 1.7 multiply_add_fusion.1
  164.1 3.4 pad.329
  167.5 3.4 pad.295
  170.8 3.4 pad.323
  174.2 1.6 multiply_add_fusion.2
  179.0 3.4 pad.290
  182.4 3.4 pad.322
  199.2 1.6 pad.317
  202.5 1.6 pad.274
  208.8 4.1 %all-to-all-start.3 = ((f32[8,32,512]{2,0,1:T(8,128)}), f32[8,32,512]{2,0,1:T(8,128)S(1)}, u32[]{:S(2)}, u32[]{:S(2)}) async-start(f32[8,32,512]{2,0,1:T(8,128)} %copy.86), calls=%async_computation.3 | async-start | bytes 1048576 | tf_op jit(solution)/shard_map/all_to_all | solution.py:80
  212.9 1.6 pad.336
  216.2 1.6 pad.319
  220.8 3.7 all-to-all-done.3
  224.7 125.7 %all-reduce.67 = (f32[256]{0:T(256)S(1)}, f32[256,16]{0,1:T(8,128)S(1)}, f32[256,16]{0,1:T(8,128)S(1)}) all-reduce(f32[256]{0:T(256)S(1)} %get-tuple-element.28, f32[256,16]{0,1:T(8,128)S(1)} %dynamic_update_slice.6, f32[256,16]{0,1:T(8,128)S(1)} %dynamic_update_slice.7), channel_id=1, replica_groups=mesh['ctx'=32,'ch'=16] {'ctx'}, use_global_device_ids=true, to_apply=%region_5.6 | all-reduce | flops 8448 | bytes 67584 | tf_op jit(solution)/shard_map/psum | solution.py:97
  352.2 29.2 %psum.36 = f32[512]{0:T(512)S(1)} all-reduce(f32[512]{0:T(512)S(1)} %get-tuple-element.29), channel_id=1, replica_groups=mesh['ctx'=32,'ch'=16] {'ch'}, use_global_device_ids=true, to_apply=%region_3.4 | all-reduce | flops 512 | bytes 4096 | tf_op jit(solution)/shard_map/psum | solution.py:92
  (291 shorter events, 88.7 us)
Async XLA Ops:
  1.7 34.5 %copy-start.28 = (bf16[512,256]{1,0:T(8,128)(2,1)S(1)}, bf16[512,256]{1,0:T(8,128)(2,1)}, u32[]{:S(2)}) copy-start(bf16[512,256]{1,0:T(8,128)(2,1)} %param.8) | copy-start | bytes 786436
  37.8 7.5 %copy-start.58 = (f32[256,16]{0,1:T(8,128)S(1)}, f32[256,16]{0,1:T(8,128)}, u32[]{:S(2)}) copy-start(f32[256,16]{0,1:T(8,128)} %param.13) | copy-start | bytes 49156
  37.8 7.5 %copy-start.59 = (f32[256,16]{0,1:T(8,128)S(1)}, f32[256,16]{0,1:T(8,128)}, u32[]{:S(2)}) copy-start(f32[256,16]{0,1:T(8,128)} %param.12) | copy-start | bytes 49156
  37.8 19.0 %all-to-all-start = ((f32[32,8,512]{2,1,0:T(8,128)}), f32[32,8,512]{2,1,0:T(8,128)S(1)}, u32[]{:S(2)}, u32[]{:S(2)}) async-start(f32[32,8,512]{2,1,0:T(8,128)} %convert_bitcast_fusion), calls=%async_computation | async-start | bytes 1048576 | tf_op jit(solution)/shard_map/all_to_all | solution.py:69
  46.1 21.2 %copy-start.50 = (f32[8,16]{1,0:T(8,128)}, f32[8,16]{1,0:T(8,128)S(1)}, u32[]{:S(2)}) copy-start(f32[8,16]{1,0:T(8,128)S(1)} %get-tuple-element.102) | copy-start | bytes 1540
  46.1 22.9 %copy-start.42 = (f32[8,16]{1,0:T(8,128)}, f32[8,16]{1,0:T(8,128)S(1)}, u32[]{:S(2)}) copy-start(f32[8,16]{1,0:T(8,128)S(1)} %get-tuple-element.103) | copy-start | bytes 1540
  46.1 24.3 %copy-start.40 = (f32[8,16]{1,0:T(8,128)}, f32[8,16]{1,0:T(8,128)S(1)}, u32[]{:S(2)}) copy-start(f32[8,16]{1,0:T(8,128)S(1)} %get-tuple-element.101) | copy-start | bytes 1540
  46.1 25.9 %copy-start.38 = (f32[8,16]{1,0:T(8,128)}, f32[8,16]{1,0:T(8,128)S(1)}, u32[]{:S(2)}) copy-start(f32[8,16]{1,0:T(8,128)S(1)} %get-tuple-element.100) | copy-start | bytes 1540
  46.3 11.0 %copy-start = (f32[8,16,128]{2,1,0:T(8,128)}, f32[8,16,128]{2,1,0:T(8,128)S(1)}, u32[]{:S(2)}) copy-start(f32[8,16,128]{2,1,0:T(8,128)S(1)} %rev.6) | copy-start | bytes 196612
  46.4 21.0 %copy-start.6 = (f32[8,1,16]{1,2,0:T(8,128)}, f32[8,1,16]{1,2,0:T(8,128)S(1)}, u32[]{:S(2)}) copy-start(f32[8,1,16]{1,2,0:T(8,128)S(1)} %copy.79) | copy-start | bytes 1540
  46.5 21.1 %copy-start.4 = (f32[8,1,16]{1,2,0:T(8,128)}, f32[8,1,16]{1,2,0:T(8,128)S(1)}, u32[]{:S(2)}) copy-start(f32[8,1,16]{1,2,0:T(8,128)S(1)} %copy.80) | copy-start | bytes 1540
  64.8 2.5 copy-start.18
  83.7 4.0 %copy-start.29 = (bf16[512,256]{1,0:T(8,128)(2,1)S(1)}, bf16[512,256]{1,0:T(8,128)(2,1)}, u32[]{:S(2)}) copy-start(bf16[512,256]{1,0:T(8,128)(2,1)} %param.9) | copy-start | bytes 786436
  83.7 15.6 %all-to-all-start.1 = ((f32[8,32,512]{2,0,1:T(8,128)}), f32[8,32,512]{2,0,1:T(8,128)S(1)}, u32[]{:S(2)}, u32[]{:S(2)}) async-start(f32[8,32,512]{2,0,1:T(8,128)} %copy.81), calls=%async_computation.1 | async-start | bytes 1048576 | tf_op jit(solution)/shard_map/all_to_all | solution.py:79
  101.3 15.5 %all-to-all-start.2 = ((f32[32,8,512]{2,1,0:T(8,128)}), f32[32,8,512]{2,1,0:T(8,128)S(1)}, u32[]{:S(2)}, u32[]{:S(2)}) async-start(f32[32,8,512]{2,1,0:T(8,128)} %get-tuple-element.62), calls=%async_computation.2 | async-start | bytes 1048576 | tf_op jit(solution)/shard_map/all_to_all | solution.py:70
  123.1 2.6 copy-start.20
  149.5 6.7 %copy-start.35 = (f32[8,2,16]{1,2,0:T(8,128)S(1)}, f32[8,2,16]{1,2,0:T(8,128)}, u32[]{:S(2)}) copy-start(f32[8,2,16]{1,2,0:T(8,128)} %get-tuple-element.56) | copy-start | bytes 3076
  152.8 6.7 %copy-start.32 = (f32[8,1,16]{1,2,0:T(8,128)S(1)}, f32[8,1,16]{1,2,0:T(8,128)}, u32[]{:S(2)}) copy-start(f32[8,1,16]{1,2,0:T(8,128)} %get-tuple-element.80) | copy-start | bytes 1540
  152.8 6.7 %copy-start.33 = (f32[8,1,16]{1,2,0:T(8,128)S(1)}, f32[8,1,16]{1,2,0:T(8,128)}, u32[]{:S(2)}) copy-start(f32[8,1,16]{1,2,0:T(8,128)} %get-tuple-element.81) | copy-start | bytes 1540
  156.2 3.4 copy-start.17
  156.2 3.4 copy-start.31
  164.1 3.4 copy-start.27
  170.8 3.4 copy-start.15
  174.2 1.6 copy-start.41
  182.4 3.4 copy-start.13
  200.9 1.6 copy-start.22
  202.5 1.6 copy-start.3
  208.8 15.7 %all-to-all-start.3 = ((f32[8,32,512]{2,0,1:T(8,128)}), f32[8,32,512]{2,0,1:T(8,128)S(1)}, u32[]{:S(2)}, u32[]{:S(2)}) async-start(f32[8,32,512]{2,0,1:T(8,128)} %copy.86), calls=%async_computation.3 | async-start | bytes 1048576 | tf_op jit(solution)/shard_map/all_to_all | solution.py:80
  212.9 1.6 copy-start.34
  214.6 1.6 copy-start.21
  220.5 4.0 %copy-start.55 = (f32[512]{0:T(512)S(1)}, f32[512]{0:T(512)}, u32[]{:S(2)}) copy-start(f32[512]{0:T(512)} %copy-done.54) | copy-start | bytes 6148
  220.5 4.0 %copy-start.57 = (f32[256]{0:T(256)S(1)}, f32[256]{0:T(256)}, u32[]{:S(2)}) copy-start(f32[256]{0:T(256)} %param.11) | copy-start | bytes 3076
  (33 other events, 27.0 us)
where the time goes:
time: 385 us; the launch traced here: 383 us
  blocking collectives  189 us (49%)
  local copies, waits for them, and re-layouts  107 us (28%)
  waiting for transfers between devices  32.3 us (8%)
  other arithmetic  21.5 us (6%)
  starting transfers between devices  19.6 us (5%)
  matrix products  11.5 us (3%)
    psum x1, blocking collectives, local(): lax.psum((residue_term, rate_term, gain_term), 'ctx')  126 us
    pad x50, local copies, waits for them, and re-layouts, local_zero(): _, states = lax.associative_scan(chain_step, (factor, contrib), axis=1)  67.3 us
    psum x1, blocking collectives, local(): square_sum = lax.psum(jnp.sum(wide_stream * wide_stream, axis=1), 'ch')  34.4 us
    psum x1, blocking collectives, local(): inner_sum = lax.psum(jnp.sum(grad_unit * unit_stream, axis=1), 'ch')  29.2 us
    slice x29, local copies, waits for them, and re-layouts, local_zero(): _, states = lax.associative_scan(chain_step, (factor, contrib), axis=1)  18.6 us
    unnamed x132, local copies, waits for them, and re-layouts  15.2 us
    all_to_all x1, waiting for transfers between devices, local(): lax.all_to_all(conv_part, 'ctx', split_axis=1, concat_axis=0, tiled=True)  9.78 us
    all_to_all x1, waiting for transfers between devices, local(): lax.all_to_all(grad_cols, 'ctx', split_axis=0, concat_axis=1, tiled=True)  9.73 us
  transfers between devices with their start and end apart: 4, of which 4 were waited for; matrix products, arithmetic and copies ran while one was open for 3% of the time, Pallas kernels for 0%

commit v1 on v0

v1 whole, which is shorter than its diff:
```python
import math

import jax
import jax.numpy as jnp
from jax import lax
from jax.experimental import pallas as pl
from jax.experimental.pallas import tpu as pltpu
from jax.sharding import PartitionSpec as P

D = 4096
MODES = 16
ROWS = 512
COLS = 256
CHUNKS = 32
CH = 16
LANES = 128
SUB = 8
BLOCKS = ROWS // SUB
HALVES = COLS // LANES
GROUPS = MODES // SUB
epsilon = 1e-05
highest = lax.Precision.HIGHEST
f32 = jnp.float32
bf16 = jnp.bfloat16


def call(kernel, outs, scratch=(), flops=1 << 22, name=None):
    return pl.pallas_call(
        kernel,
        out_shape=tuple(jax.ShapeDtypeStruct(s, d) for s, d in outs),
        scratch_shapes=list(scratch),
        cost_estimate=pl.CostEstimate(flops=flops, bytes_accessed=1 << 21, transcendentals=0),
        name=name,
    )


def lane(half):
    return pl.ds(half * LANES, LANES)


def lane_slice(half):
    return slice(half * LANES, (half + 1) * LANES)


def tiles(ref):
    return [[ref[g * SUB : (g + 1) * SUB, lane(h)] for h in range(HALVES)] for g in range(GROUPS)]


def each(fn, *args):
    return [[fn(*(a[g][h] for a in args)) for h in range(HALVES)] for g in range(GROUPS)]


def zeros_tiles():
    return [[jnp.zeros((SUB, LANES), f32) for _ in range(HALVES)] for _ in range(GROUPS)]


def fold_sublanes(parts):
    sub = lax.broadcasted_iota(jnp.int32, (SUB, LANES), 0)
    low4 = sub < 4
    low2 = (sub & 2) == 0
    low1 = (sub & 1) == 0
    four = []
    for k in range(4):
        a, b = parts[k], parts[k + 4]
        four.append(jnp.where(low4, a, b) + pltpu.roll(jnp.where(low4, b, a), 4, 0))
    two = []
    for k in range(2):
        a, b = four[k], four[k + 2]
        two.append(jnp.where(low2, a + pltpu.roll(a, 6, 0), b + pltpu.roll(b, 2, 0)))
    a, b = two
    return jnp.where(low1, a + pltpu.roll(a, 7, 0), b + pltpu.roll(b, 1, 0))


def row(ref, t, half):
    return ref[pl.ds(half * ROWS + t, SUB, stride=0), :]


def span(start, size, half):
    return (pl.ds(half * ROWS + start, size), slice(None))


def send_rows(ref, total):
    sub = lax.broadcasted_iota(jnp.int32, (SUB, LANES), 0) & 3
    parts = [total[:, k * LANES : (k + 1) * LANES] for k in range(4)]
    tile = jnp.where(
        sub == 0, parts[0], jnp.where(sub == 1, parts[1], jnp.where(sub == 2, parts[2], parts[3]))
    )
    ref[...] = jnp.broadcast_to(tile[None], (CH, SUB, LANES))


def lane_sums(values):
    ones = jnp.ones((SUB, LANES), f32)
    return lax.dot_general(
        ones, values, (((1,), (1,)), ((), ())), precision=highest, preferred_element_type=f32
    )


def columns(tile):
    turned = tile.T
    return [turned[:, k : k + 1] for k in range(4)]


def square_kernel(stream_ref, send_ref):
    wide = [stream_ref[:, lane(h)].astype(f32) for h in range(HALVES)]
    send_rows(send_ref, lane_sums(sum(v * v for v in wide)))


def adjoint_kernel(
    query_ref, grad_ref, log_rate_ref, residue_ref, g_ref, local_ref, p_ref, w_ref
):
    for h in range(HALVES):
        g_ref[span(0, ROWS, h)] = grad_ref[:, lane(h)].astype(f32) * query_ref[
            :, lane(h)
        ].astype(f32)
    lam = each(lambda v: jnp.exp(-jnp.exp(v)), tiles(log_rate_ref))
    res = tiles(residue_ref)

    def block(i, carry):
        p, w = carry
        base = pl.multiple_of((BLOCKS - 1 - i) * SUB, SUB)
        parts = [[None] * SUB for _ in range(HALVES)]
        for k in reversed(range(SUB)):
            rows = [row(g_ref, base + k, h) for h in range(HALVES)]
            a = each(lambda l, v: l * v, lam, p)
            w = each(lambda l, v, c: l * v + c, lam, w, a)
            p = [[a[g][h] + rows[h] for h in range(HALVES)] for g in range(GROUPS)]
            for h in range(HALVES):
                parts[h][k] = res[0][h] * p[0][h] + res[1][h] * p[1][h]
        for h in range(HALVES):
            local_ref[span(base, SUB, h)] = fold_sublanes(parts[h])
        return p, w

    p, w = lax.fori_loop(0, BLOCKS, block, (zeros_tiles(), zeros_tiles()))
    for g in range(GROUPS):
        for h in range(HALVES):
            p_ref[g * SUB : (g + 1) * SUB, lane(h)] = p[g][h]
            w_ref[g * SUB : (g + 1) * SUB, lane(h)] = w[g][h]


def state_kernel(
    recv_ref,
    stream_ref,
    key_ref,
    gain_ref,
    g_ref,
    local_ref,
    p_ref,
    w_ref,
    log_rate_ref,
    send_ref,
    x_ref,
    unit_ref,
    inv_ref,
    u_ref,
):
    total = jnp.sum(recv_ref[...], axis=0)
    inverse = columns(lax.rsqrt(total / D + epsilon))
    gain = gain_ref[...]
    for k in range(4):
        part = pl.ds(k * LANES, LANES)
        inv = jnp.broadcast_to(inverse[k], (LANES, LANES))
        inv_ref[part, :] = inv
        for h in range(HALVES):
            unit = stream_ref[part, lane(h)].astype(f32) * inv
            key = key_ref[part, lane(h)].astype(f32)
            own = span(k * LANES, LANES, h)
            unit_ref[own] = unit
            u_ref[own] = key * unit
            signal = key * (unit * gain[:, lane_slice(h)])
            x_ref[own] = signal.astype(bf16).astype(f32)
    lam = each(lambda v: jnp.exp(-jnp.exp(v)), tiles(log_rate_ref))

    def block(i, carry):
        state, moment, plain, first, second, gains = carry
        base = pl.multiple_of(i * SUB, SUB)
        for k in range(SUB):
            xs = [row(x_ref, base + k, h) for h in range(HALVES)]
            us = [row(u_ref, base + k, h) for h in range(HALVES)]
            gs = [row(g_ref, base + k, h) for h in range(HALVES)]
            a = each(lambda l, v: l * v, lam, state)
            moment = each(lambda l, v, c: l * v + c, lam, moment, a)
            state = [[a[g][h] + xs[h] for h in range(HALVES)] for g in range(GROUPS)]
            plain = [
                [lam[g][h] * plain[g][h] + us[h] for h in range(HALVES)] for g in range(GROUPS)
            ]
            first = [
                [first[g][h] + gs[h] * state[g][h] for h in range(HALVES)] for g in range(GROUPS)
            ]
            second = [
                [second[g][h] + gs[h] * moment[g][h] for h in range(HALVES)]
                for g in range(GROUPS)
            ]
        gains = [
            gains[h] + u_ref[span(base, SUB, h)] * local_ref[span(base, SUB, h)]
            for h in range(HALVES)
        ]
        return state, moment, plain, first, second, gains

    zero = zeros_tiles
    start = (zero(), zero(), zero(), zero(), zero(), zero()[0])
    state, moment, plain, first, second, gains = lax.fori_loop(0, BLOCKS, block, start)
    last = [gains, [jnp.zeros((SUB, LANES), f32)] * HALVES]
    sent = [state, plain, moment, tiles(p_ref), tiles(w_ref), first, second, last]
    for q in range(SUB):
        for g in range(GROUPS):
            for h in range(HALVES):
                at = g * SUB * HALVES * SUB + h * SUB + q
                send_ref[pl.ds(at, SUB, stride=HALVES * SUB), :] = sent[q][g][h]


def shifted(value, k):
    index = lax.broadcasted_iota(jnp.int32, (CHUNKS, LANES), 0)
    return jnp.where(index >= k, pltpu.roll(value, k, 0), 0.0)


def shifted_back(value, k):
    index = lax.broadcasted_iota(jnp.int32, (CHUNKS, LANES), 0)
    return jnp.where(index < CHUNKS - k, pltpu.roll(value, CHUNKS - k, 0), 0.0)


def owner_kernel(recv_ref, log_rate_ref, residue_ref, send_ref):
    state, plain, moment, p, w, first, second, gains = (
        recv_ref[pl.ds(q, CHUNKS, stride=SUB), :] for q in range(SUB)
    )
    rate = jnp.exp(log_rate_ref[...])
    res = residue_ref[...]
    lam = jnp.exp(-rate)
    whole, whole_u, whole_q, back = state, plain, moment, p
    for step in (1, 2, 4, 8, 16):
        far = jnp.exp(rate * (-float(ROWS * step)))
        before = shifted(whole, step)
        whole_q = whole_q + far * (shifted(whole_q, step) + float(ROWS * step) * before)
        whole = whole + far * before
        whole_u = whole_u + far * shifted(whole_u, step)
        back = back + far * shifted_back(back, step)
    into, into_u, into_q = shifted(whole, 1), shifted(whole_u, 1), shifted(whole_q, 1)
    into_p = shifted_back(back, 1)
    scale = 1.0 / math.sqrt(ROWS * CHUNKS)
    grad_residue = jnp.sum(first + lam * (into * p), axis=0, keepdims=True)
    weighted = jnp.sum(second + lam * ((w + p) * into + p * into_q), axis=0, keepdims=True)
    grad_gain = jnp.sum(gains + res * (lam * (into_u * p)), axis=0, keepdims=True)
    shape = (CHUNKS, LANES)
    rows = [
        into,
        into_p,
        jnp.broadcast_to(grad_residue * scale, shape),
        jnp.broadcast_to(-rate * res * weighted * scale, shape),
        jnp.broadcast_to(grad_gain * scale, shape),
    ]
    rows += [jnp.zeros(shape, f32)] * (SUB - len(rows))
    for q in range(SUB):
        send_ref[pl.ds(q, CHUNKS, stride=SUB), :] = rows[q]


def received(ref, q):
    stride = HALVES * SUB
    return [
        [
            ref[pl.ds(g * SUB * stride + h * SUB + q, SUB, stride=stride), :]
            for h in range(HALVES)
        ]
        for g in range(GROUPS)
    ]


def correct_kernel(
    recv_ref,
    local_ref,
    unit_ref,
    key_ref,
    gain_ref,
    log_rate_ref,
    residue_ref,
    send_ref,
    total_ref,
):
    lam = each(lambda v: jnp.exp(-jnp.exp(v)), tiles(log_rate_ref))
    start = each(lambda r, v: r * v, tiles(residue_ref), received(recv_ref, 1))

    def block(i, state):
        base = pl.multiple_of((BLOCKS - 1 - i) * SUB, SUB)
        parts = [[None] * SUB for _ in range(HALVES)]
        for k in reversed(range(SUB)):
            state = each(lambda l, v: l * v, lam, state)
            for h in range(HALVES):
                parts[h][k] = state[0][h] + state[1][h]
        for h in range(HALVES):
            at = span(base, SUB, h)
            total_ref[at] = local_ref[at] + fold_sublanes(parts[h])
        return state

    lax.fori_loop(0, BLOCKS, block, start)
    gain = gain_ref[...]
    products = []
    for h in range(HALVES):
        at = span(0, ROWS, h)
        grad_unit = total_ref[at] * key_ref[:, lane(h)].astype(f32) * gain[:, lane_slice(h)]
        products.append(grad_unit * unit_ref[at])
    send_rows(send_ref, lane_sums(sum(products)))


def forward_kernel(
    recv_ref,
    x_ref,
    unit_ref,
    inv_ref,
    total_ref,
    key_ref,
    query_ref,
    grad_ref,
    gain_ref,
    log_rate_ref,
    residue_ref,
    output_ref,
    grad_key_ref,
    grad_query_ref,
    left_ref,
    right_ref,
    grad_residue_ref,
    grad_rate_ref,
    grad_gain_ref,
    conv_ref,
):
    lam = each(lambda v: jnp.exp(-jnp.exp(v)), tiles(log_rate_ref))
    res = tiles(residue_ref)

    def block(i, state):
        base = pl.multiple_of(i * SUB, SUB)
        parts = [[None] * SUB for _ in range(HALVES)]
        for k in range(SUB):
            xs = [row(x_ref, base + k, h) for h in range(HALVES)]
            state = [
                [lam[g][h] * state[g][h] + xs[h] for h in range(HALVES)] for g in range(GROUPS)
            ]
            for h in range(HALVES):
                parts[h][k] = res[0][h] * state[0][h] + res[1][h] * state[1][h]
        for h in range(HALVES):
            conv_ref[span(base, SUB, h)] = fold_sublanes(parts[h])
        return state

    lax.fori_loop(0, BLOCKS, block, received(recv_ref, 0))
    gain = gain_ref[...]
    for k in range(4):
        part = pl.ds(k * LANES, LANES)
        inv = inv_ref[part, :]
        for h in range(HALVES):
            at = (part, lane(h))
            own = span(k * LANES, LANES, h)
            conv = conv_ref[own]
            output_ref[at] = (query_ref[at].astype(f32) * conv).astype(bf16)
            grad_query_ref[at] = (grad_ref[at].astype(f32) * conv).astype(bf16)
            unit = unit_ref[own]
            total = total_ref[own]
            own_gain = gain[:, lane_slice(h)]
            grad_key_ref[at] = (total * (unit * own_gain)).astype(bf16)
            left_ref[own] = inv * (total * key_ref[at].astype(f32) * own_gain)
            right_ref[own] = inv * unit
    for q, ref in ((2, grad_residue_ref), (3, grad_rate_ref)):
        found = received(recv_ref, q)
        for g in range(GROUPS):
            for h in range(HALVES):
                ref[g * SUB : (g + 1) * SUB, lane(h)] = found[g][h]
    found = received(recv_ref, 4)
    for h in range(HALVES):
        grad_gain_ref[:, lane(h)] = jnp.sum(found[0][h] + found[1][h], axis=0, keepdims=True)


def finish_kernel(recv_ref, left_ref, right_ref, grad_stream_ref):
    inner = columns(jnp.sum(recv_ref[...], axis=0) / D)
    for k in range(4):
        part = pl.ds(k * LANES, LANES)
        across = jnp.broadcast_to(inner[k], (LANES, LANES))
        for h in range(HALVES):
            own = span(k * LANES, LANES, h)
            value = left_ref[own] - right_ref[own] * across
            grad_stream_ref[part, lane(h)] = value.astype(bf16)


def exchange(value, axis):
    return lax.all_to_all(value, axis, split_axis=0, concat_axis=0, tiled=True)


def local(stream, key_gate, query_gate, grad_output, norm_gain, residue, log_rate):
    wide = (ROWS, COLS)
    split = (HALVES * ROWS, LANES)
    modes = (MODES, COLS)
    tile = (CH, SUB, LANES)
    packed = (CHUNKS * SUB, LANES)
    (squares,) = call(square_kernel, [(tile, f32)], name="square")(stream)
    squares = exchange(squares, "ch")
    log_rate_t = log_rate.T
    residue_t = residue.T
    gain = norm_gain[None, :]
    me = lax.axis_index("ctx")
    log_rate_own = lax.dynamic_slice_in_dim(log_rate_t.reshape(CHUNKS, LANES), me, 1, 0)
    residue_own = lax.dynamic_slice_in_dim(residue_t.reshape(CHUNKS, LANES), me, 1, 0)
    grad_conv, local_grad, p, w = call(
        adjoint_kernel, [(split, f32), (split, f32), (modes, f32), (modes, f32)], name="adjoint"
    )(query_gate, grad_output, log_rate_t, residue_t)
    sent, signal, unit, inv = call(
        state_kernel,
        [(packed, f32), (split, f32), (split, f32), ((ROWS, LANES), f32)],
        [pltpu.VMEM(split, f32)],
        name="state",
    )(squares, stream, key_gate, gain, grad_conv, local_grad, p, w, log_rate_t)
    got = exchange(sent.reshape(CHUNKS, SUB, LANES), "ctx").reshape(packed)
    (sent,) = call(owner_kernel, [(packed, f32)], name="owner")(got, log_rate_own, residue_own)
    got = exchange(sent.reshape(CHUNKS, SUB, LANES), "ctx").reshape(packed)
    inner, total = call(
        correct_kernel, [(tile, f32), (split, f32)], name="correct"
    )(got, local_grad, unit, key_gate, gain, log_rate_t, residue_t)
    inner = exchange(inner, "ch")
    output, grad_key, grad_query, left, right, grad_residue, grad_rate, grad_gain = call(
        forward_kernel,
        [
            (wide, bf16),
            (wide, bf16),
            (wide, bf16),
            (split, f32),
            (split, f32),
            (modes, f32),
            (modes, f32),
            ((1, COLS), f32),
        ],
        [pltpu.VMEM(split, f32)],
        name="forward",
    )(
        got,
        signal,
        unit,
        inv,
        total,
        key_gate,
        query_gate,
        grad_output,
        gain,
        log_rate_t,
        residue_t,
    )
    (grad_stream,) = call(finish_kernel, [(wide, bf16)], name="finish")(inner, left, right)
    return (
        output,
        grad_stream,
        grad_key,
        grad_query,
        grad_gain[0],
        grad_residue.T,
        grad_rate.T,
    )


def solution(mesh):
    placed = (
        P("ctx", "ch"),
        P("ctx", "ch"),
        P("ctx", "ch"),
        P("ctx", "ch"),
        P("ch"),
        P("ch", None),
        P("ch", None),
    )
    return jax.shard_map(
        local,
        mesh=mesh,
        in_specs=placed,
        out_specs=(
            P("ctx", "ch"),
            P("ctx", "ch"),
            P("ctx", "ch"),
            P("ctx", "ch"),
            P("ch"),
            P("ch", None),
            P("ch", None),
        ),
        check_vma=False,
    )
```

time: 385 us -> 90.7 us (0.24)
  the two profiles are of different devices: /device:TPU:32 before, /device:TPU:1 now
where the time goes in v1:
time: 90.7 us; the launch traced here: 90 us
  starting transfers between devices  28.9 us (32%)
  Pallas kernels  25.5 us (28%)
  waiting for transfers between devices  19.6 us (22%)
  blocking collectives  12.3 us (14%)
  local copies, waits for them, and re-layouts  3.13 us (3%)
    all_to_all x3, starting transfers between devices, exchange(): return lax.all_to_all(value, axis, split_axis=0, concat_axis=0, tiled=True)  28.9 us
    all_to_all x3, waiting for transfers between devices, exchange(): return lax.all_to_all(value, axis, split_axis=0, concat_axis=0, tiled=True)  19.6 us
    all_to_all x1, blocking collectives, exchange(): return lax.all_to_all(value, axis, split_axis=0, concat_axis=0, tiled=True)  12.3 us
    pallas_call x1, Pallas kernels, local(): call(state_kernel, [(packed, f32), (split, f32), (split, f32), ((ROWS, LA...  5.95 us
    pallas_call x1, Pallas kernels, local(): call(forward_kernel, [(wide, bf16), (wide, bf16), (wide, bf16), (split, f...  5.15 us
    pallas_call x1, Pallas kernels, local(): call(adjoint_kernel, [(split, f32), (split, f32), (modes, f32), (modes, f...  4.78 us
    pallas_call x1, Pallas kernels, local(): call(correct_kernel, [(tile, f32), (split, f32)], name='correct')  3.79 us
    unnamed x10, local copies, waits for them, and re-layouts  2.6 us
  transfers between devices with their start and end apart: 3, of which 3 were waited for; matrix products, arithmetic and copies ran while one was open for 1% of the time, Pallas kernels for 11%

profile of v1, /device:TPU:1, one launch (start us, length us, event | category | flops | bytes accessed | tf_op | source)
XLA Modules:
  0.0 90.0 jit_solution(864559964147765173)
XLA Ops:
  0.6 1.9 %square.1 = f32[16,8,128]{2,1,0:T(8,128)} custom-call(bf16[512,256]{1,0:T(8,128)(2,1)} %stream_ref.3), custom_call_target="tpu_custom_call" | custom-call | flops 4194304 | bytes 2097152 | tf_op jit(solution)/shard_map/square/pallas_call | solution.py:389
  2.6 15.7 %all-to-all-start = ((f32[16,8,128]{2,1,0:T(8,128)}), f32[16,8,128]{2,1,0:T(8,128)S(1)}, u32[]{:S(2)}, u32[]{:S(2)}) async-start(f32[16,8,128]{2,1,0:T(8,128)} %square.1), calls=%async_computation | async-start | bytes 131072 | tf_op jit(solution)/shard_map/all_to_all | solution.py:380
  18.3 4.8 %adjoint.1 = (f32[1024,128]{1,0:T(8,128)}, f32[1024,128]{1,0:T(8,128)}, f32[16,256]{1,0:T(8,128)}, f32[16,256]{1,0:T(8,128)}) custom-call(bf16[512,256]{1,0:T(8,128)(2,1)} %query_ref.3, bf16[512,256]{1,0:T(8,128)(2,1)} %grad_ref.3, f32[16,256]{1,0:T(8,128)} %bitcast.14, f32[16,256]{1,0:T(8,128)} %bitcast.19), custom_call_target="tpu_custom_call" | custom-call | flops 4194304 | bytes 2097152 | tf_op jit(solution)/shard_map/adjoint/pallas_call | solution.py:397
  23.1 6.8 %all-to-all-done.recv_ref = f32[16,8,128]{2,1,0:T(8,128)S(1)} async-done(((f32[16,8,128]{2,1,0:T(8,128)}), f32[16,8,128]{2,1,0:T(8,128)S(1)}, u32[]{:S(2)}, u32[]{:S(2)}) %all-to-all-start) | async-done | bytes 65568 | tf_op jit(solution)/shard_map/all_to_all | solution.py:380
  29.9 0.0 copy-start.3
  29.9 0.6 copy-done.3
  30.5 6.0 %state.1 = (f32[256,128]{1,0:T(8,128)}, f32[1024,128]{1,0:T(8,128)}, f32[1024,128]{1,0:T(8,128)}, f32[512,128]{1,0:T(8,128)}) custom-call(f32[16,8,128]{2,1,0:T(8,128)} %copy-done.3, bf16[512,256]{1,0:T(8,128)(2,1)} %stream_ref.3, bf16[512,256]{1,0:T(8,128)(2,1)} %key_ref.5, f32[1,256]{1,0:T(1,128)} %bitcast.24, f32[1024,128]{1,0:T(8,128)} %get-tuple-element.25.g_ref, ...), custom_call_target="tpu_custom_call" | custom-call | flops 4194304 | bytes 2097152 | tf_op jit(solution)/shard_map/state/pallas_call | solution.py:400
  36.5 0.0 copy-start.2
  36.5 9.3 %all-to-all-start.1 = ((f32[32,8,128]{2,1,0:T(8,128)}), f32[32,8,128]{2,1,0:T(8,128)S(1)}, u32[]{:S(2)}, u32[]{:S(2)}) async-start(f32[32,8,128]{2,1,0:T(8,128)} %bitcast.23), calls=%async_computation.1 | async-start | bytes 262144 | tf_op jit(solution)/shard_map/all_to_all | solution.py:380
  45.8 0.0 copy-done.2
  45.8 0.0 copy-start.1
  45.8 0.7 copy-done.1
  46.5 0.5 constant_dynamic-slice_fusion
  47.1 6.3 %all-to-all-done.1 = f32[32,8,128]{2,1,0:T(8,128)S(1)} async-done(((f32[32,8,128]{2,1,0:T(8,128)}), f32[32,8,128]{2,1,0:T(8,128)S(1)}, u32[]{:S(2)}, u32[]{:S(2)}) %all-to-all-start.1) | async-done | bytes 131104 | tf_op jit(solution)/shard_map/all_to_all | solution.py:380
  53.4 0.0 copy-start
  53.4 0.7 copy-done
  54.1 1.7 %owner.1 = f32[256,128]{1,0:T(8,128)} custom-call(f32[256,128]{1,0:T(8,128)} %bitcast.12, f32[1,128]{1,0:T(1,128)} %get-tuple-element.44.log_rate_ref, f32[1,128]{1,0:T(1,128)} %get-tuple-element.43.residue_ref), custom_call_target="tpu_custom_call" | custom-call | flops 4194304 | bytes 2097152 | tf_op jit(solution)/shard_map/owner/pallas_call | solution.py:407
  55.7 12.3 %all_to_all.20 = f32[32,8,128]{2,1,0:T(8,128)} all-to-all(f32[32,8,128]{2,1,0:T(8,128)} %bitcast.13), channel_id=1, replica_groups=mesh['ctx'=32,'ch'=16] {'ctx'}, dimensions={0} | all-to-all | bytes 262144 | tf_op jit(solution)/shard_map/all_to_all | solution.py:380
  68.0 3.8 %correct.1 = (f32[16,8,128]{2,1,0:T(8,128)}, f32[1024,128]{1,0:T(8,128)}) custom-call(f32[256,128]{1,0:T(8,128)} %bitcast.10, f32[1024,128]{1,0:T(8,128)} %get-tuple-element.26.local_ref, f32[1024,128]{1,0:T(8,128)} %get-tuple-element.31.unit_ref, bf16[512,256]{1,0:T(8,128)(2,1)} %key_ref.5, f32[1,256]{1,0:T(1,128)} %bitcast.25, f32[16,256]{1,0:T(8,128)} %bitcast.16, ...), custom_call_target="tpu_custom_call" | custom-call | flops 4194304 | bytes 2097152 | tf_op jit(solution)/shard_map/correct/pallas_call | solution.py:409
  71.8 3.8 %all-to-all-start.3 = ((f32[16,8,128]{2,1,0:T(8,128)}), f32[16,8,128]{2,1,0:T(8,128)S(1)}, u32[]{:S(2)}, u32[]{:S(2)}) async-start(f32[16,8,128]{2,1,0:T(8,128)} %get-tuple-element.35), calls=%async_computation.3 | async-start | bytes 131072 | tf_op jit(solution)/shard_map/all_to_all | solution.py:380
  75.6 5.2 %forward.1 = (bf16[512,256]{1,0:T(8,128)(2,1)}, bf16[512,256]{1,0:T(8,128)(2,1)}, bf16[512,256]{1,0:T(8,128)(2,1)}, f32[1024,128]{1,0:T(8,128)}, f32[1024,128]{1...) custom-call(f32[256,128]{1,0:T(8,128)} %bitcast.11, f32[1024,128]{1,0:T(8,128)} %get-tuple-element.30.x_ref, ...), custom_call_target="tpu_custom_call" | custom-call | flops 4194304 | bytes 2097152 | tf_op jit(solution)/shard_map/forward/pallas_call | solution.py:413
  80.8 6.4 %all-to-all-done.3.recv_ref = f32[16,8,128]{2,1,0:T(8,128)S(1)} async-done(((f32[16,8,128]{2,1,0:T(8,128)}), f32[16,8,128]{2,1,0:T(8,128)S(1)}, u32[]{:S(2)}, u32[]{:S(2)}) %all-to-all-start.3) | async-done | bytes 65568 | tf_op jit(solution)/shard_map/all_to_all | solution.py:380
  87.2 0.0 copy-start.4
  87.2 0.6 copy-done.4
  87.8 2.2 %finish.1 = bf16[512,256]{1,0:T(8,128)(2,1)} custom-call(f32[16,8,128]{2,1,0:T(8,128)} %copy-done.4, f32[1024,128]{1,0:T(8,128)} %get-tuple-element.36.left_ref, f32[1024,128]{1,0:T(8,128)} %get-tuple-element.37.right_ref), custom_call_target="tpu_custom_call" | custom-call | flops 4194304 | bytes 2097152 | tf_op jit(solution)/shard_map/finish/pallas_call | solution.py:440
  (2 shorter events, 0.0 us)
Async XLA Ops:
  2.6 27.3 %all-to-all-start = ((f32[16,8,128]{2,1,0:T(8,128)}), f32[16,8,128]{2,1,0:T(8,128)S(1)}, u32[]{:S(2)}, u32[]{:S(2)}) async-start(f32[16,8,128]{2,1,0:T(8,128)} %square.1), calls=%async_computation | async-start | bytes 131072 | tf_op jit(solution)/shard_map/all_to_all | solution.py:380
  29.9 0.6 copy-start.3
  36.5 9.4 %copy-start.2 = (f32[256,16]{0,1:T(8,128)S(1)}, f32[256,16]{0,1:T(8,128)}, u32[]{:S(2)}) copy-start(f32[256,16]{0,1:T(8,128)} %param.12) | copy-start | bytes 49156
  36.5 16.9 %all-to-all-start.1 = ((f32[32,8,128]{2,1,0:T(8,128)}), f32[32,8,128]{2,1,0:T(8,128)S(1)}, u32[]{:S(2)}, u32[]{:S(2)}) async-start(f32[32,8,128]{2,1,0:T(8,128)} %bitcast.23), calls=%async_computation.1 | async-start | bytes 262144 | tf_op jit(solution)/shard_map/all_to_all | solution.py:380
  45.8 0.7 copy-start.1
  53.4 0.7 copy-start
  71.8 15.4 %all-to-all-start.3 = ((f32[16,8,128]{2,1,0:T(8,128)}), f32[16,8,128]{2,1,0:T(8,128)S(1)}, u32[]{:S(2)}, u32[]{:S(2)}) async-start(f32[16,8,128]{2,1,0:T(8,128)} %get-tuple-element.35), calls=%async_computation.3 | async-start | bytes 131072 | tf_op jit(solution)/shard_map/all_to_all | solution.py:380
  87.2 0.6 copy-start.4

commit v2 on v1

--- a/solution.py
+++ b/solution.py
@@ -16,17 +16,20 @@
 LANES = 128
 SUB = 8
 BLOCKS = ROWS // SUB
+SPAN = 64
 HALVES = COLS // LANES
 GROUPS = MODES // SUB
 epsilon = 1e-05
-highest = lax.Precision.HIGHEST
 f32 = jnp.float32
 bf16 = jnp.bfloat16
 
 
-def call(kernel, outs, scratch=(), flops=1 << 22, name=None):
+def call(kernel, count, outs, scratch=(), flops=1 << 22, name=None):
+    held = pl.BlockSpec(memory_space=pltpu.VMEM)
     return pl.pallas_call(
         kernel,
+        in_specs=[held] * count,
+        out_specs=tuple([held] * len(outs)),
         out_shape=tuple(jax.ShapeDtypeStruct(s, d) for s, d in outs),
         scratch_shapes=list(scratch),
         cost_estimate=pl.CostEstimate(flops=flops, bytes_accessed=1 << 21, transcendentals=0),
@@ -79,20 +82,14 @@
     return (pl.ds(half * ROWS + start, size), slice(None))
 
 
-def send_rows(ref, total):
+def send_rows(ref, values):
     sub = lax.broadcasted_iota(jnp.int32, (SUB, LANES), 0) & 3
-    parts = [total[:, k * LANES : (k + 1) * LANES] for k in range(4)]
-    tile = jnp.where(
-        sub == 0, parts[0], jnp.where(sub == 1, parts[1], jnp.where(sub == 2, parts[2], parts[3]))
-    )
+    tile = None
+    for k in range(4):
+        turned = values[k * LANES : (k + 1) * LANES].T
+        part = jnp.broadcast_to(jnp.sum(turned, axis=0, keepdims=True), (SUB, LANES))
+        tile = part if tile is None else jnp.where(sub == k, part, tile)
     ref[...] = jnp.broadcast_to(tile[None], (CH, SUB, LANES))
-
-
-def lane_sums(values):
-    ones = jnp.ones((SUB, LANES), f32)
-    return lax.dot_general(
-        ones, values, (((1,), (1,)), ((), ())), precision=highest, preferred_element_type=f32
-    )
 
 
 def columns(tile):
@@ -102,32 +99,75 @@
 
 def square_kernel(stream_ref, send_ref):
     wide = [stream_ref[:, lane(h)].astype(f32) for h in range(HALVES)]
-    send_rows(send_ref, lane_sums(sum(v * v for v in wide)))
+    send_rows(send_ref, sum(v * v for v in wide))
+
+
+def tile_rows(start, group, half):
+    return pl.ds(start + (group * HALVES + half) * SUB, SUB)
 
 
 def adjoint_kernel(
-    query_ref, grad_ref, log_rate_ref, residue_ref, g_ref, local_ref, p_ref, w_ref
+    query_ref,
+    grad_ref,
+    log_rate_ref,
+    residue_ref,
+    g_ref,
+    local_ref,
+    p_ref,
+    w_ref,
+    across_ref,
+    across_lag_ref,
+    lagged_ref,
+    fade_ref,
+    rate_ref,
+    weight_ref,
 ):
     for h in range(HALVES):
         g_ref[span(0, ROWS, h)] = grad_ref[:, lane(h)].astype(f32) * query_ref[
             :, lane(h)
         ].astype(f32)
-    lam = each(lambda v: jnp.exp(-jnp.exp(v)), tiles(log_rate_ref))
+    rate = each(jnp.exp, tiles(log_rate_ref))
+    lam = each(lambda v: jnp.exp(-v), rate)
+    lam_block = each(lambda v: jnp.exp(v * (-float(SUB))), rate)
     res = tiles(residue_ref)
+    sub = lax.broadcasted_iota(jnp.int32, (SUB, LANES), 0)
 
     def block(i, carry):
         p, w = carry
-        base = pl.multiple_of((BLOCKS - 1 - i) * SUB, SUB)
+        index = BLOCKS - 1 - i
+        base = pl.multiple_of(index * SUB, SUB)
         parts = [[None] * SUB for _ in range(HALVES)]
+        near, near_w = None, None
+        far, far_w = p, w
         for k in reversed(range(SUB)):
             rows = [row(g_ref, base + k, h) for h in range(HALVES)]
-            a = each(lambda l, v: l * v, lam, p)
-            w = each(lambda l, v, c: l * v + c, lam, w, a)
-            p = [[a[g][h] + rows[h] for h in range(HALVES)] for g in range(GROUPS)]
+            p = [[lam[g][h] * p[g][h] + rows[h] for h in range(HALVES)] for g in range(GROUPS)]
             for h in range(HALVES):
                 parts[h][k] = res[0][h] * p[0][h] + res[1][h] * p[1][h]
+            if near is None:
+                near = [rows, rows]
+            else:
+                a = each(lambda l, v: l * v, lam, near)
+                if near_w is None:
+                    near_w = a
+                else:
+                    near_w = each(lambda l, v, c: l * v + c, lam, near_w, a)
+                near = [[a[g][h] + rows[h] for h in range(HALVES)] for g in range(GROUPS)]
+        w = each(
+            lambda n, l, v, q: n + l * (v + float(SUB) * q), near_w, lam_block, far_w, far
+        )
+        start = pl.multiple_of(index * (MODES * HALVES), SUB)
+        for g in range(GROUPS):
+            for h in range(HALVES):
+                at = tile_rows(start, g, h)
+                across_ref[at, :] = lam[g][h] * near[g][h]
+                across_lag_ref[at, :] = lam[g][h] * (near_w[g][h] + near[g][h])
         for h in range(HALVES):
             local_ref[span(base, SUB, h)] = fold_sublanes(parts[h])
+            own = g_ref[span(base, SUB, h)]
+            for d in range(1, SUB):
+                moved = jnp.where(sub < SUB - d, pltpu.roll(own, SUB - d, 0), 0.0)
+                lagged_ref[pl.ds((d - 1) * HALVES * ROWS + h * ROWS + base, SUB), :] = moved
         return p, w
 
     p, w = lax.fori_loop(0, BLOCKS, block, (zeros_tiles(), zeros_tiles()))
@@ -135,6 +175,19 @@
         for h in range(HALVES):
             p_ref[g * SUB : (g + 1) * SUB, lane(h)] = p[g][h]
             w_ref[g * SUB : (g + 1) * SUB, lane(h)] = w[g][h]
+            rate_ref[tile_rows(0, g, h), :] = rate[g][h]
+            weight_ref[tile_rows(0, g, h), :] = res[g][h]
+    for g in range(GROUPS):
+        for h in range(HALVES):
+            for m in range(SUB):
+                at = (g * HALVES + h) * SUB + m
+                own_rate = rate_ref[pl.ds(at, SUB, stride=0), :]
+                own_weight = weight_ref[pl.ds(at, SUB, stride=0), :]
+                for k in range(SPAN // SUB):
+                    power = (sub + (k * SUB - SPAN)).astype(f32)
+                    fade_ref[pl.ds(at * SPAN + k * SUB, SUB), :] = own_weight * jnp.exp(
+                        own_rate * power
+                    )
 
 
 def state_kernel(
@@ -146,11 +199,15 @@
     local_ref,
     p_ref,
     w_ref,
+    across_ref,
+    across_lag_ref,
+    lagged_ref,
     log_rate_ref,
     send_ref,
     x_ref,
     unit_ref,
     inv_ref,
+    full_ref,
     u_ref,
 ):
     total = jnp.sum(recv_ref[...], axis=0)
@@ -167,38 +224,68 @@
             unit_ref[own] = unit
             u_ref[own] = key * unit
             signal = key * (unit * gain[:, lane_slice(h)])
+            full_ref[own] = signal
             x_ref[own] = signal.astype(bf16).astype(f32)
     lam = each(lambda v: jnp.exp(-jnp.exp(v)), tiles(log_rate_ref))
 
     def block(i, carry):
-        state, moment, plain, first, second, gains = carry
+        state, moment, plain, first, second = carry
         base = pl.multiple_of(i * SUB, SUB)
+        start = pl.multiple_of(i * (MODES * HALVES), SUB)
+        near = [[across_ref[tile_rows(start, g, h), :] for h in range(HALVES)] for g in range(GROUPS)]
+        near_lag = [
+            [across_lag_ref[tile_rows(start, g, h), :] for h in range(HALVES)]
+            for g in range(GROUPS)
+        ]
+        first = each(lambda f, s, n: f + s * n, first, state, near)
+        second = each(
+            lambda f, s, n, m, v: f + (s * n + m * v), second, state, near_lag, moment, near
+        )
         for k in range(SUB):
             xs = [row(x_ref, base + k, h) for h in range(HALVES)]
             us = [row(u_ref, base + k, h) for h in range(HALVES)]
-            gs = [row(g_ref, base + k, h) for h in range(HALVES)]
             a = each(lambda l, v: l * v, lam, state)
             moment = each(lambda l, v, c: l * v + c, lam, moment, a)
             state = [[a[g][h] + xs[h] for h in range(HALVES)] for g in range(GROUPS)]
             plain = [
                 [lam[g][h] * plain[g][h] + us[h] for h in range(HALVES)] for g in range(GROUPS)
             ]
-            first = [
-                [first[g][h] + gs[h] * state[g][h] for h in range(HALVES)] for g in range(GROUPS)
-            ]
-            second = [
-                [second[g][h] + gs[h] * moment[g][h] for h in range(HALVES)]
-                for g in range(GROUPS)
-            ]
-        gains = [
-            gains[h] + u_ref[span(base, SUB, h)] * local_ref[span(base, SUB, h)]
+        return state, moment, plain, first, second
+
+    zero = zeros_tiles
+    start = (zero(), zero(), zero(), zero(), zero())
+    state, moment, plain, first, second = lax.fori_loop(0, BLOCKS, block, start)
+
+    def inside(i, carry):
+        sums, gains = carry
+        base = pl.multiple_of(i * SUB, SUB)
+        new_sums, new_gains = [], []
+        for h in range(HALVES):
+            at = span(base, SUB, h)
+            x = x_ref[at]
+            new_gains.append(gains[h] + u_ref[at] * local_ref[at])
+            own = [sums[h][0] + x * g_ref[at]]
+            for d in range(1, SUB):
+                moved = lagged_ref[pl.ds((d - 1) * HALVES * ROWS + h * ROWS + base, SUB), :]
+                own.append(sums[h][d] + x * moved)
+            new_sums.append(own)
+        return new_sums, new_gains
+
+    none = jnp.zeros((SUB, LANES), f32)
+    sums, gains = lax.fori_loop(
+        0, BLOCKS, inside, ([[none] * SUB for _ in range(HALVES)], [none] * HALVES), unroll=2
+    )
+    near, near_lag = zero(), zero()
+    for d in reversed(range(SUB)):
+        each_sum = [
+            jnp.broadcast_to(jnp.sum(sums[h][d], axis=0, keepdims=True), (SUB, LANES))
             for h in range(HALVES)
         ]
-        return state, moment, plain, first, second, gains
-
-    zero = zeros_tiles
-    start = (zero(), zero(), zero(), zero(), zero(), zero()[0])
-    state, moment, plain, first, second, gains = lax.fori_loop(0, BLOCKS, block, start)
+        a = each(lambda l, v: l * v, lam, near)
+        near_lag = each(lambda l, v, c: l * v + c, lam, near_lag, a)
+        near = [[a[g][h] + each_sum[h] for h in range(HALVES)] for g in range(GROUPS)]
+    first = each(lambda f, n: f + n, first, near)
+    second = each(lambda f, n: f + n, second, near_lag)
     last = [gains, [jnp.zeros((SUB, LANES), f32)] * HALVES]
     sent = [state, plain, moment, tiles(p_ref), tiles(w_ref), first, second, last]
     for q in range(SUB):
@@ -266,37 +353,40 @@
 def correct_kernel(
     recv_ref,
     local_ref,
-    unit_ref,
-    key_ref,
-    gain_ref,
+    full_ref,
+    fade_ref,
     log_rate_ref,
-    residue_ref,
     send_ref,
     total_ref,
+    into_ref,
 ):
-    lam = each(lambda v: jnp.exp(-jnp.exp(v)), tiles(log_rate_ref))
-    start = each(lambda r, v: r * v, tiles(residue_ref), received(recv_ref, 1))
-
-    def block(i, state):
-        base = pl.multiple_of((BLOCKS - 1 - i) * SUB, SUB)
-        parts = [[None] * SUB for _ in range(HALVES)]
-        for k in reversed(range(SUB)):
-            state = each(lambda l, v: l * v, lam, state)
+    into = received(recv_ref, 1)
+    step = each(lambda v: jnp.exp(jnp.exp(v) * (-float(SPAN))), tiles(log_rate_ref))
+    spans = ROWS // SPAN
+    for b in reversed(range(spans)):
+        for g in range(GROUPS):
             for h in range(HALVES):
-                parts[h][k] = state[0][h] + state[1][h]
-        for h in range(HALVES):
-            at = span(base, SUB, h)
-            total_ref[at] = local_ref[at] + fold_sublanes(parts[h])
-        return state
-
-    lax.fori_loop(0, BLOCKS, block, start)
-    gain = gain_ref[...]
-    products = []
-    for h in range(HALVES):
-        at = span(0, ROWS, h)
-        grad_unit = total_ref[at] * key_ref[:, lane(h)].astype(f32) * gain[:, lane_slice(h)]
-        products.append(grad_unit * unit_ref[at])
-    send_rows(send_ref, lane_sums(sum(products)))
+                into_ref[tile_rows(b * MODES * HALVES, g, h), :] = into[g][h]
+        into = each(lambda l, v: l * v, step, into)
+
+    def block(b, carry):
+        for h in range(HALVES):
+            places = [(g * HALVES + h) * SUB + m for g in range(GROUPS) for m in range(SUB)]
+            rows = [into_ref[pl.ds(b * MODES * HALVES + at, SUB, stride=0), :] for at in places]
+            for k in range(SPAN // SUB):
+                own = span(pl.multiple_of(b * SPAN + k * SUB, SUB), SUB, h)
+                terms = [
+                    fade_ref[pl.ds(at * SPAN + k * SUB, SUB), :] * rows[m]
+                    for m, at in enumerate(places)
+                ]
+                while len(terms) > 1:
+                    terms = [a + b for a, b in zip(terms[::2], terms[1::2])]
+                total_ref[own] = local_ref[own] + terms[0]
+        return carry
+
+    lax.fori_loop(0, spans, block, 0)
+    products = [total_ref[span(0, ROWS, h)] * full_ref[span(0, ROWS, h)] for h in range(HALVES)]
+    send_rows(send_ref, sum(products))
 
 
 def forward_kernel(
@@ -386,7 +476,7 @@
     modes = (MODES, COLS)
     tile = (CH, SUB, LANES)
     packed = (CHUNKS * SUB, LANES)
-    (squares,) = call(square_kernel, [(tile, f32)], name="square")(stream)
+    (squares,) = call(square_kernel, 1, [(tile, f32)], name="square")(stream)
     squares = exchange(squares, "ch")
     log_rate_t = log_rate.T
     residue_t = residue.T
@@ -394,24 +484,58 @@
     me = lax.axis_index("ctx")
     log_rate_own = lax.dynamic_slice_in_dim(log_rate_t.reshape(CHUNKS, LANES), me, 1, 0)
     residue_own = lax.dynamic_slice_in_dim(residue_t.reshape(CHUNKS, LANES), me, 1, 0)
-    grad_conv, local_grad, p, w = call(
-        adjoint_kernel, [(split, f32), (split, f32), (modes, f32), (modes, f32)], name="adjoint"
+    table = (BLOCKS * MODES * HALVES, LANES)
+    few = (MODES * HALVES, LANES)
+    grad_conv, local_grad, p, w, across, across_lag, lagged, fade = call(
+        adjoint_kernel,
+        4,
+        [
+            (split, f32),
+            (split, f32),
+            (modes, f32),
+            (modes, f32),
+            (table, f32),
+            (table, f32),
+            (((SUB - 1) * HALVES * ROWS, LANES), f32),
+            ((MODES * HALVES * SPAN, LANES), f32),
+        ],
+        [pltpu.VMEM(few, f32), pltpu.VMEM(few, f32)],
+        name="adjoint",
     )(query_gate, grad_output, log_rate_t, residue_t)
-    sent, signal, unit, inv = call(
+    sent, signal, unit, inv, full = call(
         state_kernel,
-        [(packed, f32), (split, f32), (split, f32), ((ROWS, LANES), f32)],
+        12,
+        [(packed, f32), (split, f32), (split, f32), ((ROWS, LANES), f32), (split, f32)],
         [pltpu.VMEM(split, f32)],
         name="state",
-    )(squares, stream, key_gate, gain, grad_conv, local_grad, p, w, log_rate_t)
+    )(
+        squares,
+        stream,
+        key_gate,
+        gain,
+        grad_conv,
+        local_grad,
+        p,
+        w,
+        across,
+        across_lag,
+        lagged,
+        log_rate_t,
+    )
     got = exchange(sent.reshape(CHUNKS, SUB, LANES), "ctx").reshape(packed)
-    (sent,) = call(owner_kernel, [(packed, f32)], name="owner")(got, log_rate_own, residue_own)
+    (sent,) = call(owner_kernel, 3, [(packed, f32)], name="owner")(got, log_rate_own, residue_own)
     got = exchange(sent.reshape(CHUNKS, SUB, LANES), "ctx").reshape(packed)
     inner, total = call(
-        correct_kernel, [(tile, f32), (split, f32)], name="correct"
-    )(got, local_grad, unit, key_gate, gain, log_rate_t, residue_t)
+        correct_kernel,
+        5,
+        [(tile, f32), (split, f32)],
+        [pltpu.VMEM((ROWS // SPAN * MODES * HALVES, LANES), f32)],
+        name="correct",
+    )(got, local_grad, full, fade, log_rate_t)
     inner = exchange(inner, "ch")
     output, grad_key, grad_query, left, right, grad_residue, grad_rate, grad_gain = call(
         forward_kernel,
+        11,
         [
             (wide, bf16),
             (wide, bf16),
@@ -437,7 +561,7 @@
         log_rate_t,
         residue_t,
     )
-    (grad_stream,) = call(finish_kernel, [(wide, bf16)], name="finish")(inner, left, right)
+    (grad_stream,) = call(finish_kernel, 3, [(wide, bf16)], name="finish")(inner, left, right)
     return (
         output,
         grad_stream,

time: 90.7 us -> 94.2 us (1.039)
  Pallas kernels: 25.5 us -> 29.3 us
  starting transfers between devices: 28.9 us -> 31.6 us
  waiting for transfers between devices: 19.6 us -> 17.4 us
    pallas_call x7, Pallas kernels: 25.5 us -> 29.3 us  [the longest x1 7.8 us: local(): call(state_kernel, 12, [(packed, f32), (split, f32), (split, f32), ((ROWS...]
    all_to_all x3, starting transfers between devices: 28.9 us -> 31.6 us  [exchange(): return lax.all_to_all(value, axis, split_axis=0, concat_axis=0, tiled=True)]
    all_to_all x3, waiting for transfers between devices: 19.6 us -> 17.4 us  [exchange(): return lax.all_to_all(value, axis, split_axis=0, concat_axis=0, tiled=True)]
  transfers between devices with their start and end apart: 3 -> 3, of which waited for: 3 -> 3; matrix products, arithmetic and copies ran while one was open for 1% -> 1% of each run, Pallas kernels for 11% -> 14%
where the time goes in v2:
time: 94.2 us; the launch traced here: 93.7 us
  starting transfers between devices  31.6 us (34%)
  Pallas kernels  29.3 us (31%)
  waiting for transfers between devices  17.4 us (18%)
  blocking collectives  12.3 us (13%)
  local copies, waits for them, and re-layouts  2.44 us (3%)
    all_to_all x3, starting transfers between devices, exchange(): return lax.all_to_all(value, axis, split_axis=0, concat_axis=0, tiled=True)  31.6 us
    all_to_all x3, waiting for transfers between devices, exchange(): return lax.all_to_all(value, axis, split_axis=0, concat_axis=0, tiled=True)  17.4 us
    all_to_all x1, blocking collectives, exchange(): return lax.all_to_all(value, axis, split_axis=0, concat_axis=0, tiled=True)  12.3 us
    pallas_call x1, Pallas kernels, local(): call(state_kernel, 12, [(packed, f32), (split, f32), (split, f32), ((ROWS...  7.8 us
    pallas_call x1, Pallas kernels, local(): call(adjoint_kernel, 4, [(split, f32), (split, f32), (modes, f32), (modes...  7.66 us
    pallas_call x1, Pallas kernels, local(): call(forward_kernel, 11, [(wide, bf16), (wide, bf16), (wide, bf16), (spli...  5.15 us
    pallas_call x1, Pallas kernels, local(): call(correct_kernel, 5, [(tile, f32), (split, f32)], [pltpu.VMEM((ROWS //...  3.04 us
    pallas_call x1, Pallas kernels, local(): call(finish_kernel, 3, [(wide, bf16)], name='finish')(inner, left, right)  2.19 us
  transfers between devices with their start and end apart: 3, of which 3 were waited for; matrix products, arithmetic and copies ran while one was open for 1% of the time, Pallas kernels for 14%

profile of v2, /device:TPU:1, one launch (start us, length us, event | category | flops | bytes accessed | tf_op | source)
XLA Modules:
  0.0 93.7 jit_solution(18088332035516404229)
XLA Ops:
  0.6 1.7 %square.1 = f32[16,8,128]{2,1,0:T(8,128)} custom-call(bf16[512,256]{1,0:T(8,128)(2,1)} %stream_ref.3), custom_call_target="tpu_custom_call" | custom-call | flops 4194304 | bytes 2097152 | tf_op jit(solution)/shard_map/square/pallas_call | solution.py:479
  2.4 15.7 %all-to-all-start = ((f32[16,8,128]{2,1,0:T(8,128)}), f32[16,8,128]{2,1,0:T(8,128)S(1)}, u32[]{:S(2)}, u32[]{:S(2)}) async-start(f32[16,8,128]{2,1,0:T(8,128)} %square.1), calls=%async_computation | async-start | bytes 131072 | tf_op jit(solution)/shard_map/all_to_all | solution.py:470
  18.1 7.7 %adjoint.1 = (f32[1024,128]{1,0:T(8,128)}, f32[1024,128]{1,0:T(8,128)}, f32[16,256]{1,0:T(8,128)}, f32[16,256]{1,0:T(8,128)}, f32[2048,128]{1,0:T(8,128)}, /*ind...) custom-call(bf16[512,256]{1,0:T(8,128)(2,1)} %query_ref.3, bf16[512,256]{1,0:T(8,128)(2,1)} %grad_ref.3, ...), custom_call_target="tpu_custom_call" | custom-call | flops 4194304 | bytes 2097152 | tf_op jit(solution)/shard_map/adjoint/pallas_call | solution.py:489
  25.8 3.9 %all-to-all-done.recv_ref = f32[16,8,128]{2,1,0:T(8,128)S(1)} async-done(((f32[16,8,128]{2,1,0:T(8,128)}), f32[16,8,128]{2,1,0:T(8,128)S(1)}, u32[]{:S(2)}, u32[]{:S(2)}) %all-to-all-start) | async-done | bytes 65568 | tf_op jit(solution)/shard_map/all_to_all | solution.py:470
  29.7 0.0 copy-start.2
  29.7 0.6 copy-done.2
  30.3 0.0 copy-start.1
  30.3 0.0 copy-start.4
  30.3 7.8 %state.1 = (f32[256,128]{1,0:T(8,128)}, f32[1024,128]{1,0:T(8,128)}, f32[1024,128]{1,0:T(8,128)}, f32[512,128]{1,0:T(8,128)}, f32[1024,128]{1,0:T(8,128)}) custom-call(f32[16,8,128]{2,1,0:T(8,128)} %copy-done.2, bf16[512,256]{1,0:T(8,128)(2,1)} %stream_ref.3, bf16[512,256]{1,0:T(8,128)(2,1)} %key_ref.3, f32[1,256]{1,0:T(1,128)} %bitcast.23, ...), custom_call_target="tpu_custom_call" | custom-call | flops 4194304 | bytes 2097152 | tf_op jit(solution)/shard_map/state/pallas_call | solution.py:505
  38.1 9.2 %all-to-all-start.1 = ((f32[32,8,128]{2,1,0:T(8,128)}), f32[32,8,128]{2,1,0:T(8,128)S(1)}, u32[]{:S(2)}, u32[]{:S(2)}) async-start(f32[32,8,128]{2,1,0:T(8,128)} %bitcast.22), calls=%async_computation.1 | async-start | bytes 262144 | tf_op jit(solution)/shard_map/all_to_all | solution.py:470
  47.3 0.0 copy-done.1
  47.3 0.0 copy-done.4
  47.4 0.5 constant_dynamic-slice_fusion
  47.9 7.0 %all-to-all-done.1 = f32[32,8,128]{2,1,0:T(8,128)S(1)} async-done(((f32[32,8,128]{2,1,0:T(8,128)}), f32[32,8,128]{2,1,0:T(8,128)S(1)}, u32[]{:S(2)}, u32[]{:S(2)}) %all-to-all-start.1) | async-done | bytes 131104 | tf_op jit(solution)/shard_map/all_to_all | solution.py:470
  54.9 0.0 copy-start
  54.9 0.7 copy-done
  55.6 1.7 %owner.1 = f32[256,128]{1,0:T(8,128)} custom-call(f32[256,128]{1,0:T(8,128)} %bitcast.12, f32[1,128]{1,0:T(1,128)} %get-tuple-element.54.log_rate_ref, f32[1,128]{1,0:T(1,128)} %get-tuple-element.53.residue_ref), custom_call_target="tpu_custom_call" | custom-call | flops 4194304 | bytes 2097152 | tf_op jit(solution)/shard_map/owner/pallas_call | solution.py:526
  57.2 12.3 %all_to_all.20 = f32[32,8,128]{2,1,0:T(8,128)} all-to-all(f32[32,8,128]{2,1,0:T(8,128)} %bitcast.13), channel_id=1, replica_groups=mesh['ctx'=32,'ch'=16] {'ctx'}, dimensions={0} | all-to-all | bytes 262144 | tf_op jit(solution)/shard_map/all_to_all | solution.py:470
  69.6 3.0 %correct.1 = (f32[16,8,128]{2,1,0:T(8,128)}, f32[1024,128]{1,0:T(8,128)}) custom-call(f32[256,128]{1,0:T(8,128)} %bitcast.10, f32[1024,128]{1,0:T(8,128)} %get-tuple-element.31.local_ref, f32[1024,128]{1,0:T(8,128)} %get-tuple-element.41.full_ref, f32[2048,128]{1,0:T(8,128)} %get-tuple-element.42.fade_ref, f32[16,256]{1,0:T(8,128)} %bitcast.16), custom_call_target="tpu_custom_call" | custom-call | flops 4194304 | bytes 2097152 | tf_op jit(solution)/shard_map/correct/pallas_call | solution.py:528
  72.6 6.7 %all-to-all-start.3 = ((f32[16,8,128]{2,1,0:T(8,128)}), f32[16,8,128]{2,1,0:T(8,128)S(1)}, u32[]{:S(2)}, u32[]{:S(2)}) async-start(f32[16,8,128]{2,1,0:T(8,128)} %get-tuple-element.45), calls=%async_computation.3 | async-start | bytes 131072 | tf_op jit(solution)/shard_map/all_to_all | solution.py:470
  79.3 5.2 %forward.1 = (bf16[512,256]{1,0:T(8,128)(2,1)}, bf16[512,256]{1,0:T(8,128)(2,1)}, bf16[512,256]{1,0:T(8,128)(2,1)}, f32[1024,128]{1,0:T(8,128)}, f32[1024,128]{1...) custom-call(f32[256,128]{1,0:T(8,128)} %bitcast.11, f32[1024,128]{1,0:T(8,128)} %get-tuple-element.38.x_ref, ...), custom_call_target="tpu_custom_call" | custom-call | flops 4194304 | bytes 2097152 | tf_op jit(solution)/shard_map/forward/pallas_call | solution.py:536
  84.4 6.4 %all-to-all-done.3.recv_ref = f32[16,8,128]{2,1,0:T(8,128)S(1)} async-done(((f32[16,8,128]{2,1,0:T(8,128)}), f32[16,8,128]{2,1,0:T(8,128)S(1)}, u32[]{:S(2)}, u32[]{:S(2)}) %all-to-all-start.3) | async-done | bytes 65568 | tf_op jit(solution)/shard_map/all_to_all | solution.py:470
  90.9 0.0 copy-start.3
  90.9 0.6 copy-done.3
  91.5 2.2 %finish.1 = bf16[512,256]{1,0:T(8,128)(2,1)} custom-call(f32[16,8,128]{2,1,0:T(8,128)} %copy-done.3, f32[1024,128]{1,0:T(8,128)} %get-tuple-element.46.left_ref, f32[1024,128]{1,0:T(8,128)} %get-tuple-element.47.right_ref), custom_call_target="tpu_custom_call" | custom-call | flops 4194304 | bytes 2097152 | tf_op jit(solution)/shard_map/finish/pallas_call | solution.py:564
  (2 shorter events, 0.0 us)
Async XLA Ops:
  2.4 27.3 %all-to-all-start = ((f32[16,8,128]{2,1,0:T(8,128)}), f32[16,8,128]{2,1,0:T(8,128)S(1)}, u32[]{:S(2)}, u32[]{:S(2)}) async-start(f32[16,8,128]{2,1,0:T(8,128)} %square.1), calls=%async_computation | async-start | bytes 131072 | tf_op jit(solution)/shard_map/all_to_all | solution.py:470
  29.7 0.6 copy-start.2
  30.3 17.0 %copy-start.1 = (f32[256,16]{0,1:T(8,128)S(1)}, f32[256,16]{0,1:T(8,128)}, u32[]{:S(2)}) copy-start(f32[256,16]{0,1:T(8,128)} %param.13) | copy-start | bytes 49156
  30.3 17.0 %copy-start.4 = (f32[256,16]{0,1:T(8,128)S(1)}, f32[256,16]{0,1:T(8,128)}, u32[]{:S(2)}) copy-start(f32[256,16]{0,1:T(8,128)} %param.12) | copy-start | bytes 49156
  38.1 16.8 %all-to-all-start.1 = ((f32[32,8,128]{2,1,0:T(8,128)}), f32[32,8,128]{2,1,0:T(8,128)S(1)}, u32[]{:S(2)}, u32[]{:S(2)}) async-start(f32[32,8,128]{2,1,0:T(8,128)} %bitcast.22), calls=%async_computation.1 | async-start | bytes 262144 | tf_op jit(solution)/shard_map/all_to_all | solution.py:470
  54.9 0.7 copy-start
  72.6 18.3 %all-to-all-start.3 = ((f32[16,8,128]{2,1,0:T(8,128)}), f32[16,8,128]{2,1,0:T(8,128)S(1)}, u32[]{:S(2)}, u32[]{:S(2)}) async-start(f32[16,8,128]{2,1,0:T(8,128)} %get-tuple-element.45), calls=%async_computation.3 | async-start | bytes 131072 | tf_op jit(solution)/shard_map/all_to_all | solution.py:470
  90.9 0.6 copy-start.3

commit v3 on v2

--- a/solution.py
+++ b/solution.py
@@ -16,7 +16,7 @@
 LANES = 128
 SUB = 8
 BLOCKS = ROWS // SUB
-SPAN = 64
+SPAN = 32
 HALVES = COLS // LANES
 GROUPS = MODES // SUB
 epsilon = 1e-05
@@ -24,14 +24,17 @@
 bf16 = jnp.bfloat16
 
 
-def call(kernel, count, outs, scratch=(), flops=1 << 22, name=None):
-    held = pl.BlockSpec(memory_space=pltpu.VMEM)
+def call(kernel, ins, outs, scratch=(), limit=8, flops=1 << 22, name=None):
+    held = {"v": pl.BlockSpec(memory_space=pltpu.VMEM), "a": pl.BlockSpec(memory_space=pltpu.HBM)}
     return pl.pallas_call(
         kernel,
-        in_specs=[held] * count,
-        out_specs=tuple([held] * len(outs)),
-        out_shape=tuple(jax.ShapeDtypeStruct(s, d) for s, d in outs),
+        in_specs=[held[k] for k in ins],
+        out_specs=tuple(held[k] for _, _, k in outs),
+        out_shape=tuple(
+            pltpu.HBM(s, d) if k == "a" else jax.ShapeDtypeStruct(s, d) for s, d, k in outs
+        ),
         scratch_shapes=list(scratch),
+        compiler_params=pltpu.CompilerParams(vmem_limit_bytes=limit << 20),
         cost_estimate=pl.CostEstimate(flops=flops, bytes_accessed=1 << 21, transcendentals=0),
         name=name,
     )
@@ -111,17 +114,18 @@
     grad_ref,
     log_rate_ref,
     residue_ref,
+    gain_ref,
     g_ref,
-    local_ref,
+    local_out,
     p_ref,
     w_ref,
     across_ref,
     across_lag_ref,
-    lagged_ref,
-    fade_ref,
-    rate_ref,
-    weight_ref,
+    gain_out,
+    local_ref,
+    done,
 ):
+    gain_out[...] = gain_ref[...]
     for h in range(HALVES):
         g_ref[span(0, ROWS, h)] = grad_ref[:, lane(h)].astype(f32) * query_ref[
             :, lane(h)
@@ -130,7 +134,6 @@
     lam = each(lambda v: jnp.exp(-v), rate)
     lam_block = each(lambda v: jnp.exp(v * (-float(SUB))), rate)
     res = tiles(residue_ref)
-    sub = lax.broadcasted_iota(jnp.int32, (SUB, LANES), 0)
 
     def block(i, carry):
         p, w = carry
@@ -164,30 +167,37 @@
                 across_lag_ref[at, :] = lam[g][h] * (near_w[g][h] + near[g][h])
         for h in range(HALVES):
             local_ref[span(base, SUB, h)] = fold_sublanes(parts[h])
-            own = g_ref[span(base, SUB, h)]
-            for d in range(1, SUB):
-                moved = jnp.where(sub < SUB - d, pltpu.roll(own, SUB - d, 0), 0.0)
-                lagged_ref[pl.ds((d - 1) * HALVES * ROWS + h * ROWS + base, SUB), :] = moved
         return p, w
 
     p, w = lax.fori_loop(0, BLOCKS, block, (zeros_tiles(), zeros_tiles()))
+    copy = pltpu.make_async_copy(local_ref, local_out, done)
+    copy.start()
     for g in range(GROUPS):
         for h in range(HALVES):
             p_ref[g * SUB : (g + 1) * SUB, lane(h)] = p[g][h]
             w_ref[g * SUB : (g + 1) * SUB, lane(h)] = w[g][h]
+    copy.wait()
+
+
+def fade_kernel(log_rate_ref, residue_ref, after_ref, fade_ref, rate_ref, weight_ref):
+    sub = lax.broadcasted_iota(jnp.int32, (SUB, LANES), 0)
+    rate = each(jnp.exp, tiles(log_rate_ref))
+    res = tiles(residue_ref)
+    for g in range(GROUPS):
+        for h in range(HALVES):
             rate_ref[tile_rows(0, g, h), :] = rate[g][h]
             weight_ref[tile_rows(0, g, h), :] = res[g][h]
-    for g in range(GROUPS):
-        for h in range(HALVES):
-            for m in range(SUB):
-                at = (g * HALVES + h) * SUB + m
-                own_rate = rate_ref[pl.ds(at, SUB, stride=0), :]
-                own_weight = weight_ref[pl.ds(at, SUB, stride=0), :]
-                for k in range(SPAN // SUB):
-                    power = (sub + (k * SUB - SPAN)).astype(f32)
-                    fade_ref[pl.ds(at * SPAN + k * SUB, SUB), :] = own_weight * jnp.exp(
-                        own_rate * power
-                    )
+
+    def block(at, carry):
+        own_rate = rate_ref[pl.ds(at, SUB, stride=0), :]
+        own_weight = weight_ref[pl.ds(at, SUB, stride=0), :]
+        for k in range(SPAN // SUB):
+            power = (sub + (k * SUB - SPAN)).astype(f32)
+            rows = pl.ds(pl.multiple_of(at * SPAN + k * SUB, SUB), SUB)
+            fade_ref[rows, :] = own_weight * jnp.exp(own_rate * power)
+        return carry
+
+    lax.fori_loop(0, MODES * HALVES, block, 0, unroll=4)
 
 
 def state_kernel(
@@ -196,20 +206,27 @@
     key_ref,
     gain_ref,
     g_ref,
-    local_ref,
+    local_in,
     p_ref,
     w_ref,
     across_ref,
     across_lag_ref,
-    lagged_ref,
     log_rate_ref,
+    send_out,
+    signal_out,
+    inv_out,
+    full_out,
     send_ref,
-    x_ref,
-    unit_ref,
+    signal_ref,
     inv_ref,
     full_ref,
+    local_ref,
+    x_ref,
     u_ref,
+    done,
 ):
+    fetch = pltpu.make_async_copy(local_in, local_ref, done.at[0])
+    fetch.start()
     total = jnp.sum(recv_ref[...], axis=0)
     inverse = columns(lax.rsqrt(total / D + epsilon))
     gain = gain_ref[...]
@@ -221,11 +238,19 @@
             unit = stream_ref[part, lane(h)].astype(f32) * inv
             key = key_ref[part, lane(h)].astype(f32)
             own = span(k * LANES, LANES, h)
-            unit_ref[own] = unit
             u_ref[own] = key * unit
             signal = key * (unit * gain[:, lane_slice(h)])
             full_ref[own] = signal
-            x_ref[own] = signal.astype(bf16).astype(f32)
+            narrow = signal.astype(bf16)
+            signal_ref[own] = narrow
+            x_ref[own] = narrow.astype(f32)
+    stores = [
+        pltpu.make_async_copy(signal_ref, signal_out, done.at[1]),
+        pltpu.make_async_copy(inv_ref, inv_out, done.at[2]),
+        pltpu.make_async_copy(full_ref, full_out, done.at[3]),
+    ]
+    for copy in stores:
+        copy.start()
     lam = each(lambda v: jnp.exp(-jnp.exp(v)), tiles(log_rate_ref))
 
     def block(i, carry):
@@ -256,6 +281,8 @@
     start = (zero(), zero(), zero(), zero(), zero())
     state, moment, plain, first, second = lax.fori_loop(0, BLOCKS, block, start)
 
+    sub = lax.broadcasted_iota(jnp.int32, (SUB, LANES), 0)
+
     def inside(i, carry):
         sums, gains = carry
         base = pl.multiple_of(i * SUB, SUB)
@@ -264,13 +291,15 @@
             at = span(base, SUB, h)
             x = x_ref[at]
             new_gains.append(gains[h] + u_ref[at] * local_ref[at])
-            own = [sums[h][0] + x * g_ref[at]]
+            later = g_ref[at]
+            own = [sums[h][0] + x * later]
             for d in range(1, SUB):
-                moved = lagged_ref[pl.ds((d - 1) * HALVES * ROWS + h * ROWS + base, SUB), :]
+                moved = jnp.where(sub < SUB - d, pltpu.roll(later, SUB - d, 0), 0.0)
                 own.append(sums[h][d] + x * moved)
             new_sums.append(own)
         return new_sums, new_gains
 
+    fetch.wait()
     none = jnp.zeros((SUB, LANES), f32)
     sums, gains = lax.fori_loop(
         0, BLOCKS, inside, ([[none] * SUB for _ in range(HALVES)], [none] * HALVES), unroll=2
@@ -288,11 +317,17 @@
     second = each(lambda f, n: f + n, second, near_lag)
     last = [gains, [jnp.zeros((SUB, LANES), f32)] * HALVES]
     sent = [state, plain, moment, tiles(p_ref), tiles(w_ref), first, second, last]
+    flat_ref = send_ref.reshape(CHUNKS * SUB, LANES)
     for q in range(SUB):
         for g in range(GROUPS):
             for h in range(HALVES):
                 at = g * SUB * HALVES * SUB + h * SUB + q
-                send_ref[pl.ds(at, SUB, stride=HALVES * SUB), :] = sent[q][g][h]
+                flat_ref[pl.ds(at, SUB, stride=HALVES * SUB), :] = sent[q][g][h]
+    copy = pltpu.make_async_copy(send_ref, send_out, done.at[4])
+    copy.start()
+    for store in stores:
+        store.wait()
+    copy.wait()
 
 
 def shifted(value, k):
@@ -306,8 +341,9 @@
 
 
 def owner_kernel(recv_ref, log_rate_ref, residue_ref, send_ref):
+    flat_ref = recv_ref.reshape(CHUNKS * SUB, LANES)
     state, plain, moment, p, w, first, second, gains = (
-        recv_ref[pl.ds(q, CHUNKS, stride=SUB), :] for q in range(SUB)
+        flat_ref[pl.ds(q, CHUNKS, stride=SUB), :] for q in range(SUB)
     )
     rate = jnp.exp(log_rate_ref[...])
     res = residue_ref[...]
@@ -335,15 +371,17 @@
         jnp.broadcast_to(grad_gain * scale, shape),
     ]
     rows += [jnp.zeros(shape, f32)] * (SUB - len(rows))
+    flat_ref = send_ref.reshape(CHUNKS * SUB, LANES)
     for q in range(SUB):
-        send_ref[pl.ds(q, CHUNKS, stride=SUB), :] = rows[q]
+        flat_ref[pl.ds(q, CHUNKS, stride=SUB), :] = rows[q]
 
 
 def received(ref, q):
     stride = HALVES * SUB
+    flat_ref = ref.reshape(CHUNKS * SUB, LANES)
     return [
         [
-            ref[pl.ds(g * SUB * stride + h * SUB + q, SUB, stride=stride), :]
+            flat_ref[pl.ds(g * SUB * stride + h * SUB + q, SUB, stride=stride), :]
             for h in range(HALVES)
         ]
         for g in range(GROUPS)
@@ -357,8 +395,10 @@
     fade_ref,
     log_rate_ref,
     send_ref,
+    total_out,
+    into_ref,
     total_ref,
-    into_ref,
+    done,
 ):
     into = received(recv_ref, 1)
     step = each(lambda v: jnp.exp(jnp.exp(v) * (-float(SPAN))), tiles(log_rate_ref))
@@ -385,16 +425,19 @@
         return carry
 
     lax.fori_loop(0, spans, block, 0)
+    copy = pltpu.make_async_copy(total_ref, total_out, done)
+    copy.start()
     products = [total_ref[span(0, ROWS, h)] * full_ref[span(0, ROWS, h)] for h in range(HALVES)]
     send_rows(send_ref, sum(products))
+    copy.wait()
 
 
 def forward_kernel(
     recv_ref,
-    x_ref,
-    unit_ref,
+    signal_ref,
     inv_ref,
     total_ref,
+    stream_ref,
     key_ref,
     query_ref,
     grad_ref,
@@ -410,7 +453,9 @@
     grad_rate_ref,
     grad_gain_ref,
     conv_ref,
+    x_ref,
 ):
+    x_ref[...] = signal_ref[...].astype(f32)
     lam = each(lambda v: jnp.exp(-jnp.exp(v)), tiles(log_rate_ref))
     res = tiles(residue_ref)
 
@@ -439,7 +484,7 @@
             conv = conv_ref[own]
             output_ref[at] = (query_ref[at].astype(f32) * conv).astype(bf16)
             grad_query_ref[at] = (grad_ref[at].astype(f32) * conv).astype(bf16)
-            unit = unit_ref[own]
+            unit = stream_ref[at].astype(f32) * inv
             total = total_ref[own]
             own_gain = gain[:, lane_slice(h)]
             grad_key_ref[at] = (total * (unit * own_gain)).astype(bf16)
@@ -466,6 +511,10 @@
             grad_stream_ref[part, lane(h)] = value.astype(bf16)
 
 
+def in_hbm(value):
+    return pltpu.with_memory_space_constraint(value, pltpu.HBM)
+
+
 def exchange(value, axis):
     return lax.all_to_all(value, axis, split_axis=0, concat_axis=0, tiled=True)
 
@@ -475,38 +524,46 @@
     split = (HALVES * ROWS, LANES)
     modes = (MODES, COLS)
     tile = (CH, SUB, LANES)
-    packed = (CHUNKS * SUB, LANES)
-    (squares,) = call(square_kernel, 1, [(tile, f32)], name="square")(stream)
+    (squares,) = call(square_kernel, "v", [(tile, f32, "v")], name="square")(stream)
     squares = exchange(squares, "ch")
     log_rate_t = log_rate.T
     residue_t = residue.T
-    gain = norm_gain[None, :]
     me = lax.axis_index("ctx")
     log_rate_own = lax.dynamic_slice_in_dim(log_rate_t.reshape(CHUNKS, LANES), me, 1, 0)
     residue_own = lax.dynamic_slice_in_dim(residue_t.reshape(CHUNKS, LANES), me, 1, 0)
     table = (BLOCKS * MODES * HALVES, LANES)
     few = (MODES * HALVES, LANES)
-    grad_conv, local_grad, p, w, across, across_lag, lagged, fade = call(
+    packed = (CHUNKS, SUB, LANES)
+    grad_conv, local_grad, p, w, across, across_lag, gain = call(
         adjoint_kernel,
-        4,
+        "vvvvv",
         [
-            (split, f32),
-            (split, f32),
-            (modes, f32),
-            (modes, f32),
-            (table, f32),
-            (table, f32),
-            (((SUB - 1) * HALVES * ROWS, LANES), f32),
-            ((MODES * HALVES * SPAN, LANES), f32),
+            (split, f32, "v"),
+            (split, f32, "a"),
+            (modes, f32, "v"),
+            (modes, f32, "v"),
+            (table, f32, "v"),
+            (table, f32, "v"),
+            ((1, COLS), f32, "v"),
         ],
-        [pltpu.VMEM(few, f32), pltpu.VMEM(few, f32)],
+        [pltpu.VMEM(split, f32), pltpu.SemaphoreType.DMA],
         name="adjoint",
-    )(query_gate, grad_output, log_rate_t, residue_t)
-    sent, signal, unit, inv, full = call(
+    )(query_gate, grad_output, log_rate_t, residue_t, norm_gain[None, :])
+    rows = (ROWS, LANES)
+    sent, signal, inv, full = call(
         state_kernel,
-        12,
-        [(packed, f32), (split, f32), (split, f32), ((ROWS, LANES), f32), (split, f32)],
-        [pltpu.VMEM(split, f32)],
+        "vvvvvavvvvv",
+        [(packed, f32, "a"), (split, bf16, "a"), (rows, f32, "a"), (split, f32, "a")],
+        [
+            pltpu.VMEM(packed, f32),
+            pltpu.VMEM(split, bf16),
+            pltpu.VMEM(rows, f32),
+            pltpu.VMEM(split, f32),
+            pltpu.VMEM(split, f32),
+            pltpu.VMEM(split, f32),
+            pltpu.VMEM(split, f32),
+            pltpu.SemaphoreType.DMA((5,)),
+        ],
         name="state",
     )(
         squares,
@@ -514,46 +571,58 @@
         key_gate,
         gain,
         grad_conv,
-        local_grad,
+        in_hbm(local_grad),
         p,
         w,
         across,
         across_lag,
-        lagged,
         log_rate_t,
     )
-    got = exchange(sent.reshape(CHUNKS, SUB, LANES), "ctx").reshape(packed)
-    (sent,) = call(owner_kernel, 3, [(packed, f32)], name="owner")(got, log_rate_own, residue_own)
-    got = exchange(sent.reshape(CHUNKS, SUB, LANES), "ctx").reshape(packed)
+    got = exchange(sent, "ctx")
+    (fade,) = call(
+        fade_kernel,
+        "vva",
+        [((MODES * HALVES * SPAN, LANES), f32, "v")],
+        [pltpu.VMEM(few, f32), pltpu.VMEM(few, f32)],
+        name="fade",
+    )(log_rate_t, residue_t, in_hbm(inv))
+    (sent,) = call(owner_kernel, "vvv", [(packed, f32, "v")], name="owner")(
+        got, log_rate_own, residue_own
+    )
+    got = exchange(sent, "ctx")
     inner, total = call(
         correct_kernel,
-        5,
-        [(tile, f32), (split, f32)],
-        [pltpu.VMEM((ROWS // SPAN * MODES * HALVES, LANES), f32)],
+        "vvvvv",
+        [(tile, f32, "v"), (split, f32, "a")],
+        [
+            pltpu.VMEM((ROWS // SPAN * MODES * HALVES, LANES), f32),
+            pltpu.VMEM(split, f32),
+            pltpu.SemaphoreType.DMA,
+        ],
         name="correct",
     )(got, local_grad, full, fade, log_rate_t)
     inner = exchange(inner, "ch")
     output, grad_key, grad_query, left, right, grad_residue, grad_rate, grad_gain = call(
         forward_kernel,
-        11,
+        "v" * 11,
         [
-            (wide, bf16),
-            (wide, bf16),
-            (wide, bf16),
-            (split, f32),
-            (split, f32),
-            (modes, f32),
-            (modes, f32),
-            ((1, COLS), f32),
+            (wide, bf16, "v"),
+            (wide, bf16, "v"),
+            (wide, bf16, "v"),
+            (split, f32, "v"),
+            (split, f32, "v"),
+            (modes, f32, "v"),
+            (modes, f32, "v"),
+            ((1, COLS), f32, "v"),
         ],
-        [pltpu.VMEM(split, f32)],
+        [pltpu.VMEM(split, f32), pltpu.VMEM(split, f32)],
         name="forward",
     )(
         got,
         signal,
-        unit,
         inv,
         total,
+        stream,
         key_gate,
         query_gate,
         grad_output,
@@ -561,7 +630,7 @@
         log_rate_t,
         residue_t,
     )
-    (grad_stream,) = call(finish_kernel, 3, [(wide, bf16)], name="finish")(inner, left, right)
+    (grad_stream,) = call(finish_kernel, "vvv", [(wide, bf16, "v")], name="finish")(inner, left, right)
     return (
         output,
         grad_stream,

time: 94.2 us -> 83.4 us (0.89)
  Pallas kernels: 29.3 us -> 16.2 us
  blocking collectives: 12.3 us -> 0 us
  waiting for transfers between devices: 17.4 us -> 28.4 us
  starting transfers between devices: 31.6 us -> 33.9 us
  local copies, waits for them, and re-layouts: 2.44 us -> 3.63 us
    pallas_call x7 -> x8, Pallas kernels: 29.3 us -> 16.2 us  [the longest x1 4.09 us: local(): call(state_kernel, 'vvvvvavvvvv', [(packed, f32, 'a'), (split, bf16, 'a')...]
    all_to_all x1 -> x0, blocking collectives: 12.3 us -> none  [exchange(): return lax.all_to_all(value, axis, split_axis=0, concat_axis=0, tiled=True)]
    all_to_all x3 -> x4, waiting for transfers between devices: 17.4 us -> 28.4 us  [exchange(): return lax.all_to_all(value, axis, split_axis=0, concat_axis=0, tiled=True)]
    all_to_all x3 -> x4, starting transfers between devices: 31.6 us -> 33.9 us  [exchange(): return lax.all_to_all(value, axis, split_axis=0, concat_axis=0, tiled=True)]
    unnamed x10 -> x28, local copies, waits for them, and re-layouts: 1.91 us -> 3.61 us
  transfers between devices with their start and end apart: 3 -> 4, of which waited for: 3 -> 4; matrix products, arithmetic and copies ran while one was open for 1% -> 0% of each run, Pallas kernels for 14% -> 9%
where the time goes in v3:
time: 83.4 us; the launch traced here: 82.9 us
  starting transfers between devices  33.9 us (41%)
  waiting for transfers between devices  28.4 us (34%)
  Pallas kernels  16.2 us (19%)
  local copies, waits for them, and re-layouts  3.63 us (4%)
    all_to_all x4, starting transfers between devices, exchange(): return lax.all_to_all(value, axis, split_axis=0, concat_axis=0, tiled=True)  33.9 us
    all_to_all x4, waiting for transfers between devices, exchange(): return lax.all_to_all(value, axis, split_axis=0, concat_axis=0, tiled=True)  28.4 us
    pallas_call x1, Pallas kernels, local(): call(state_kernel, 'vvvvvavvvvv', [(packed, f32, 'a'), (split, bf16, 'a')...  4.09 us
    pallas_call x1, Pallas kernels, local(): call(adjoint_kernel, 'vvvvv', [(split, f32, 'v'), (split, f32, 'a'), (mod...  4.03 us
    unnamed x28, local copies, waits for them, and re-layouts  3.61 us
    pallas_call x1, Pallas kernels, local(): call(forward_kernel, 'v' * 11, [(wide, bf16, 'v'), (wide, bf16, 'v'), (wi...  3.09 us
    pallas_call x1, Pallas kernels, local(): call(correct_kernel, 'vvvvv', [(tile, f32, 'v'), (split, f32, 'a')], [plt...  2.28 us
  transfers between devices with their start and end apart: 4, of which 4 were waited for; matrix products, arithmetic and copies ran while one was open for 0% of the time, Pallas kernels for 9%

profile of v3, /device:TPU:1, one launch (start us, length us, event | category | flops | bytes accessed | tf_op | source)
XLA Modules:
  0.0 82.9 jit_solution(4838274463678280943)
XLA Ops:
  0.6 0.0 copy-start
  0.6 0.9 %copy-done = bf16[512,256]{1,0:T(8,128)(2,1)S(1)} copy-done((bf16[512,256]{1,0:T(8,128)(2,1)S(1)}, bf16[512,256]{1,0:T(8,128)(2,1)}, u32[]{:S(2)}) %copy-start) | copy-done | bytes 262168
  1.6 0.8 square.1
  2.4 15.9 %all-to-all-start = ((f32[16,8,128]{2,1,0:T(8,128)}), f32[16,8,128]{2,1,0:T(8,128)S(1)}, u32[]{:S(2)}, u32[]{:S(2)}) async-start(f32[16,8,128]{2,1,0:T(8,128)} %square.1), calls=%async_computation | async-start | bytes 131072 | tf_op jit(solution)/shard_map/all_to_all | solution.py:519
  18.2 0.0 copy-start.13
  18.3 0.0 copy-done.5
  18.3 0.0 copy-done.8
  18.3 0.0 copy-done.11
  18.3 0.6 copy-done.13
  18.9 0.9 %copy-done.6 = bf16[512,256]{1,0:T(8,128)(2,1)S(1)} copy-done((bf16[512,256]{1,0:T(8,128)(2,1)S(1)}, bf16[512,256]{1,0:T(8,128)(2,1)}, u32[]{:S(2)}) %copy-start.6) | copy-done | bytes 262168
  19.9 4.0 %adjoint.1 = (f32[1024,128]{1,0:T(8,128)S(1)}, f32[1024,128]{1,0:T(8,128)}, f32[16,256]{1,0:T(8,128)S(1)}, f32[16,256]{1,0:T(8,128)S(1)}, f32[2048,128]{1,0:T(8,...) custom-call(bf16[512,256]{1,0:T(8,128)(2,1)S(1)} %copy-done.5, bf16[512,256]{1,0:T(8,128)(2,1)S(1)} %copy-done.6, ...), custom_call_target="tpu_custom_call" | custom-call | flops 4194304 | bytes 2097152 | tf_op jit(solution)/shard_map/adjoint/pallas_call | solution.py:537
  23.9 5.9 %all-to-all-done.recv_ref = f32[16,8,128]{2,1,0:T(8,128)S(1)} async-done(((f32[16,8,128]{2,1,0:T(8,128)}), f32[16,8,128]{2,1,0:T(8,128)S(1)}, u32[]{:S(2)}, u32[]{:S(2)}) %all-to-all-start) | async-done | bytes 65568 | tf_op jit(solution)/shard_map/all_to_all | solution.py:519
  29.8 0.0 copy-done.1
  29.8 0.0 copy-done.3
  29.8 4.1 %state.1 = (f32[32,8,128]{2,1,0:T(8,128)}, bf16[1024,128]{1,0:T(8,128)(2,1)}, f32[512,128]{1,0:T(8,128)}, f32[1024,128]{1,0:T(8,128)}) custom-call(f32[16,8,128]{2,1,0:T(8,128)S(1)} %all-to-all-done.recv_ref, bf16[512,256]{1,0:T(8,128)(2,1)S(1)} %copy-done.1, bf16[512,256]{1,0:T(8,128)(2,1)S(1)} %copy-done.3, f32[1,256]{1,0:T(1,128)S(1)} %get-tuple-element.28.gain_ref, ...), custom_call_target="tpu_custom_call" | custom-call | flops 4194304 | bytes 2097152 | tf_op jit(solution)/shard_map/state/pallas_call | solution.py:553
  33.9 9.2 %all-to-all-start.1 = ((f32[32,8,128]{2,1,0:T(8,128)}), f32[32,8,128]{2,1,0:T(8,128)S(1)}, u32[]{:S(2)}, u32[]{:S(2)}) async-start(f32[32,8,128]{2,1,0:T(8,128)} %get-tuple-element.35), calls=%async_computation.1 | async-start | bytes 262144 | tf_op jit(solution)/shard_map/all_to_all | solution.py:519
  43.2 7.6 %all-to-all-done.1.recv_ref = f32[32,8,128]{2,1,0:T(8,128)S(1)} async-done(((f32[32,8,128]{2,1,0:T(8,128)}), f32[32,8,128]{2,1,0:T(8,128)S(1)}, u32[]{:S(2)}, u32[]{:S(2)}) %all-to-all-start.1) | async-done | bytes 131104 | tf_op jit(solution)/shard_map/all_to_all | solution.py:519
  50.7 0.7 owner.1
  51.5 4.1 %all-to-all-start.2 = ((f32[32,8,128]{2,1,0:T(8,128)}), f32[32,8,128]{2,1,0:T(8,128)S(1)}, u32[]{:S(2)}, u32[]{:S(2)}) async-start(f32[32,8,128]{2,1,0:T(8,128)} %owner.1), calls=%async_computation.2 | async-start | bytes 262144 | tf_op jit(solution)/shard_map/all_to_all | solution.py:519
  55.5 0.2 fade.1.fade_ref
  55.7 7.5 %all-to-all-done.2.recv_ref = f32[32,8,128]{2,1,0:T(8,128)S(1)} async-done(((f32[32,8,128]{2,1,0:T(8,128)}), f32[32,8,128]{2,1,0:T(8,128)S(1)}, u32[]{:S(2)}, u32[]{:S(2)}) %all-to-all-start.2) | async-done | bytes 131104 | tf_op jit(solution)/shard_map/all_to_all | solution.py:519
  63.3 0.0 copy-done.2
  63.3 0.0 copy-done.9
  63.3 0.0 copy-start.12
  63.3 2.3 %correct.1 = (f32[16,8,128]{2,1,0:T(8,128)}, f32[1024,128]{1,0:T(8,128)}) custom-call(f32[32,8,128]{2,1,0:T(8,128)S(1)} %all-to-all-done.2.recv_ref, f32[1024,128]{1,0:T(8,128)S(1)} %copy-done.2, f32[1024,128]{1,0:T(8,128)S(1)} %copy-done.9, f32[1024,128]{1,0:T(8,128)S(1)} %fade.1.fade_ref, f32[16,256]{1,0:T(8,128)S(1)} %bitcast.10), custom_call_target="tpu_custom_call" | custom-call | flops 4194304 | bytes 2097152 | tf_op jit(solution)/shard_map/correct/pallas_call | solution.py:593
  65.6 4.7 %all-to-all-start.3 = ((f32[16,8,128]{2,1,0:T(8,128)}), f32[16,8,128]{2,1,0:T(8,128)S(1)}, u32[]{:S(2)}, u32[]{:S(2)}) async-start(f32[16,8,128]{2,1,0:T(8,128)} %get-tuple-element.41), calls=%async_computation.3 | async-start | bytes 131072 | tf_op jit(solution)/shard_map/all_to_all | solution.py:519
  70.3 0.0 copy-done.4
  70.3 0.0 copy-done.7
  70.3 1.0 %copy-done.10 = f32[1024,128]{1,0:T(8,128)S(1)} copy-done((f32[1024,128]{1,0:T(8,128)S(1)}, f32[1024,128]{1,0:T(8,128)}, u32[]{:S(2)}) %copy-start.10) | copy-done | bytes 524312
  71.4 3.1 %forward.1 = (bf16[512,256]{1,0:T(8,128)(2,1)}, bf16[512,256]{1,0:T(8,128)(2,1)}, bf16[512,256]{1,0:T(8,128)(2,1)}, f32[1024,128]{1,0:T(8,128)S(1)}, f32[1024,12...) custom-call(f32[32,8,128]{2,1,0:T(8,128)S(1)} %all-to-all-done.2.recv_ref, ...), custom_call_target="tpu_custom_call" | custom-call | flops 4194304 | bytes 2097152 | tf_op jit(solution)/shard_map/forward/pallas_call | solution.py:605
  74.5 7.4 %all-to-all-done.3.recv_ref = f32[16,8,128]{2,1,0:T(8,128)S(1)} async-done(((f32[16,8,128]{2,1,0:T(8,128)}), f32[16,8,128]{2,1,0:T(8,128)S(1)}, u32[]{:S(2)}, u32[]{:S(2)}) %all-to-all-start.3) | async-done | bytes 65568 | tf_op jit(solution)/shard_map/all_to_all | solution.py:519
  81.9 1.0 %finish.1 = bf16[512,256]{1,0:T(8,128)(2,1)} custom-call(f32[16,8,128]{2,1,0:T(8,128)S(1)} %all-to-all-done.3.recv_ref, f32[1024,128]{1,0:T(8,128)S(1)} %get-tuple-element.42.left_ref, f32[1024,128]{1,0:T(8,128)S(1)} %get-tuple-element.43.right_ref), custom_call_target="tpu_custom_call" | custom-call | flops 4194304 | bytes 2097152 | tf_op jit(solution)/shard_map/finish/pallas_call | solution.py:633
  (15 shorter events, 0.0 us)
Async XLA Ops:
  0.6 1.0 %copy-start = (bf16[512,256]{1,0:T(8,128)(2,1)S(1)}, bf16[512,256]{1,0:T(8,128)(2,1)}, u32[]{:S(2)}) copy-start(bf16[512,256]{1,0:T(8,128)(2,1)} %stream_ref.5) | copy-start | bytes 786436
  1.6 16.7 %copy-start.5 = (bf16[512,256]{1,0:T(8,128)(2,1)S(1)}, bf16[512,256]{1,0:T(8,128)(2,1)}, u32[]{:S(2)}) copy-start(bf16[512,256]{1,0:T(8,128)(2,1)} %query_ref.3) | copy-start | bytes 786436
  2.4 15.9 %copy-start.8 = (f32[256,16]{0,1:T(8,128)S(1)}, f32[256,16]{0,1:T(8,128)}, u32[]{:S(2)}) copy-start(f32[256,16]{0,1:T(8,128)} %param.13) | copy-start | bytes 49156
  2.4 15.9 %copy-start.11 = (f32[256,16]{0,1:T(8,128)S(1)}, f32[256,16]{0,1:T(8,128)}, u32[]{:S(2)}) copy-start(f32[256,16]{0,1:T(8,128)} %param.12) | copy-start | bytes 49156
  2.4 27.4 %all-to-all-start = ((f32[16,8,128]{2,1,0:T(8,128)}), f32[16,8,128]{2,1,0:T(8,128)S(1)}, u32[]{:S(2)}, u32[]{:S(2)}) async-start(f32[16,8,128]{2,1,0:T(8,128)} %square.1), calls=%async_computation | async-start | bytes 131072 | tf_op jit(solution)/shard_map/all_to_all | solution.py:519
  18.2 0.7 copy-start.13
  18.9 0.9 %copy-start.6 = (bf16[512,256]{1,0:T(8,128)(2,1)S(1)}, bf16[512,256]{1,0:T(8,128)(2,1)}, u32[]{:S(2)}) copy-start(bf16[512,256]{1,0:T(8,128)(2,1)} %grad_ref.3) | copy-start | bytes 786436
  19.9 9.9 %copy-start.1 = (bf16[512,256]{1,0:T(8,128)(2,1)S(1)}, bf16[512,256]{1,0:T(8,128)(2,1)}, u32[]{:S(2)}) copy-start(bf16[512,256]{1,0:T(8,128)(2,1)} %stream_ref.5) | copy-start | bytes 786436
  19.9 9.9 %copy-start.3 = (bf16[512,256]{1,0:T(8,128)(2,1)S(1)}, bf16[512,256]{1,0:T(8,128)(2,1)}, u32[]{:S(2)}) copy-start(bf16[512,256]{1,0:T(8,128)(2,1)} %key_ref.3) | copy-start | bytes 786436
  33.9 16.8 %all-to-all-start.1 = ((f32[32,8,128]{2,1,0:T(8,128)}), f32[32,8,128]{2,1,0:T(8,128)S(1)}, u32[]{:S(2)}, u32[]{:S(2)}) async-start(f32[32,8,128]{2,1,0:T(8,128)} %get-tuple-element.35), calls=%async_computation.1 | async-start | bytes 262144 | tf_op jit(solution)/shard_map/all_to_all | solution.py:519
  51.5 11.8 %copy-start.2 = (f32[1024,128]{1,0:T(8,128)S(1)}, f32[1024,128]{1,0:T(8,128)}, u32[]{:S(2)}) copy-start(f32[1024,128]{1,0:T(8,128)} %get-tuple-element.30.local_in.local_ref) | copy-start | bytes 1572868
  51.5 11.8 %copy-start.9 = (f32[1024,128]{1,0:T(8,128)S(1)}, f32[1024,128]{1,0:T(8,128)}, u32[]{:S(2)}) copy-start(f32[1024,128]{1,0:T(8,128)} %get-tuple-element.38.full_ref) | copy-start | bytes 1572868
  51.5 11.8 %all-to-all-start.2 = ((f32[32,8,128]{2,1,0:T(8,128)}), f32[32,8,128]{2,1,0:T(8,128)S(1)}, u32[]{:S(2)}, u32[]{:S(2)}) async-start(f32[32,8,128]{2,1,0:T(8,128)} %owner.1), calls=%async_computation.2 | async-start | bytes 262144 | tf_op jit(solution)/shard_map/all_to_all | solution.py:519
  63.3 7.0 %copy-start.4 = (f32[512,128]{1,0:T(8,128)S(1)}, f32[512,128]{1,0:T(8,128)}, u32[]{:S(2)}) copy-start(f32[512,128]{1,0:T(8,128)} %get-tuple-element.37.after_ref.inv_ref) | copy-start | bytes 786436
  63.3 7.1 %copy-start.7 = (bf16[512,256]{1,0:T(8,128)(2,1)S(1)}, bf16[512,256]{1,0:T(8,128)(2,1)}, u32[]{:S(2)}) copy-start(bf16[512,256]{1,0:T(8,128)(2,1)} %grad_ref.3) | copy-start | bytes 786436
  63.3 7.1 %copy-start.12 = (bf16[1024,128]{1,0:T(8,128)(2,1)S(1)}, bf16[1024,128]{1,0:T(8,128)(2,1)}, u32[]{:S(2)}) copy-start(bf16[1024,128]{1,0:T(8,128)(2,1)} %get-tuple-element.36.signal_ref) | copy-start | bytes 786436
  65.6 16.3 %all-to-all-start.3 = ((f32[16,8,128]{2,1,0:T(8,128)}), f32[16,8,128]{2,1,0:T(8,128)S(1)}, u32[]{:S(2)}, u32[]{:S(2)}) async-start(f32[16,8,128]{2,1,0:T(8,128)} %get-tuple-element.41), calls=%async_computation.3 | async-start | bytes 131072 | tf_op jit(solution)/shard_map/all_to_all | solution.py:519
  70.3 1.0 %copy-start.10 = (f32[1024,128]{1,0:T(8,128)S(1)}, f32[1024,128]{1,0:T(8,128)}, u32[]{:S(2)}) copy-start(f32[1024,128]{1,0:T(8,128)} %get-tuple-element.39.total_ref) | copy-start | bytes 1572868

commit v4 on v3

--- a/solution.py
+++ b/solution.py
@@ -16,7 +16,8 @@
 LANES = 128
 SUB = 8
 BLOCKS = ROWS // SUB
-SPAN = 32
+SPAN = 16
+QUARTERS = ROWS // LANES
 HALVES = COLS // LANES
 GROUPS = MODES // SUB
 epsilon = 1e-05
@@ -85,13 +86,15 @@
     return (pl.ds(half * ROWS + start, size), slice(None))
 
 
-def send_rows(ref, values):
+def lane_totals(values):
+    return jnp.broadcast_to(jnp.sum(values.T, axis=0, keepdims=True), (SUB, LANES))
+
+
+def send_rows(ref, parts):
     sub = lax.broadcasted_iota(jnp.int32, (SUB, LANES), 0) & 3
-    tile = None
-    for k in range(4):
-        turned = values[k * LANES : (k + 1) * LANES].T
-        part = jnp.broadcast_to(jnp.sum(turned, axis=0, keepdims=True), (SUB, LANES))
-        tile = part if tile is None else jnp.where(sub == k, part, tile)
+    tile = parts[0]
+    for k in range(1, QUARTERS):
+        tile = jnp.where(sub == k, parts[k], tile)
     ref[...] = jnp.broadcast_to(tile[None], (CH, SUB, LANES))
 
 
@@ -101,8 +104,12 @@
 
 
 def square_kernel(stream_ref, send_ref):
-    wide = [stream_ref[:, lane(h)].astype(f32) for h in range(HALVES)]
-    send_rows(send_ref, sum(v * v for v in wide))
+    parts = []
+    for k in range(QUARTERS):
+        part = pl.ds(k * LANES, LANES)
+        wide = [stream_ref[part, lane(h)].astype(f32) for h in range(HALVES)]
+        parts.append(lane_totals(sum(v * v for v in wide)))
+    send_rows(send_ref, parts)
 
 
 def tile_rows(start, group, half):
@@ -115,21 +122,32 @@
     log_rate_ref,
     residue_ref,
     gain_ref,
-    g_ref,
+    own_log_rate_ref,
+    own_residue_ref,
+    g_out,
     local_out,
     p_ref,
     w_ref,
     across_ref,
     across_lag_ref,
     gain_out,
+    own_log_rate_out,
+    own_residue_out,
+    g_ref,
     local_ref,
     done,
 ):
     gain_out[...] = gain_ref[...]
+    own_log_rate_out[...] = own_log_rate_ref[...]
+    own_residue_out[...] = own_residue_ref[...]
     for h in range(HALVES):
         g_ref[span(0, ROWS, h)] = grad_ref[:, lane(h)].astype(f32) * query_ref[
             :, lane(h)
         ].astype(f32)
+    g_copy = pltpu.make_async_copy(
+        g_ref.reshape(HALVES * BLOCKS, SUB, LANES), g_out, done.at[1]
+    )
+    g_copy.start()
     rate = each(jnp.exp, tiles(log_rate_ref))
     lam = each(lambda v: jnp.exp(-v), rate)
     lam_block = each(lambda v: jnp.exp(v * (-float(SUB))), rate)
@@ -170,16 +188,17 @@
         return p, w
 
     p, w = lax.fori_loop(0, BLOCKS, block, (zeros_tiles(), zeros_tiles()))
-    copy = pltpu.make_async_copy(local_ref, local_out, done)
+    copy = pltpu.make_async_copy(local_ref, local_out, done.at[0])
     copy.start()
     for g in range(GROUPS):
         for h in range(HALVES):
             p_ref[g * SUB : (g + 1) * SUB, lane(h)] = p[g][h]
             w_ref[g * SUB : (g + 1) * SUB, lane(h)] = w[g][h]
     copy.wait()
-
-
-def fade_kernel(log_rate_ref, residue_ref, after_ref, fade_ref, rate_ref, weight_ref):
+    g_copy.wait()
+
+
+def fill_fade(log_rate_ref, residue_ref, fade_ref, rate_ref, weight_ref):
     sub = lax.broadcasted_iota(jnp.int32, (SUB, LANES), 0)
     rate = each(jnp.exp, tiles(log_rate_ref))
     res = tiles(residue_ref)
@@ -197,7 +216,7 @@
             fade_ref[rows, :] = own_weight * jnp.exp(own_rate * power)
         return carry
 
-    lax.fori_loop(0, MODES * HALVES, block, 0, unroll=4)
+    lax.fori_loop(0, MODES * HALVES, block, 0, unroll=8)
 
 
 def state_kernel(
@@ -205,28 +224,30 @@
     stream_ref,
     key_ref,
     gain_ref,
-    g_ref,
+    g_in,
     local_in,
     p_ref,
     w_ref,
     across_ref,
     across_lag_ref,
     log_rate_ref,
-    send_out,
+    send_ref,
     signal_out,
     inv_out,
-    full_out,
-    send_ref,
+    full_ref,
     signal_ref,
     inv_ref,
-    full_ref,
     local_ref,
     x_ref,
     u_ref,
+    padded_ref,
     done,
 ):
     fetch = pltpu.make_async_copy(local_in, local_ref, done.at[0])
     fetch.start()
+    wider_ref = padded_ref.reshape(HALVES * BLOCKS, 2 * SUB, LANES)
+    fetch_g = pltpu.make_async_copy(g_in, wider_ref.at[:, pl.ds(0, SUB), :], done.at[3])
+    fetch_g.start()
     total = jnp.sum(recv_ref[...], axis=0)
     inverse = columns(lax.rsqrt(total / D + epsilon))
     gain = gain_ref[...]
@@ -247,7 +268,6 @@
     stores = [
         pltpu.make_async_copy(signal_ref, signal_out, done.at[1]),
         pltpu.make_async_copy(inv_ref, inv_out, done.at[2]),
-        pltpu.make_async_copy(full_ref, full_out, done.at[3]),
     ]
     for copy in stores:
         copy.start()
@@ -266,6 +286,9 @@
         second = each(
             lambda f, s, n, m, v: f + (s * n + m * v), second, state, near_lag, moment, near
         )
+        for h in range(HALVES):
+            wider = pl.multiple_of((h * BLOCKS + i) * 2 * SUB, 2 * SUB)
+            padded_ref[pl.ds(wider + SUB, SUB), :] = jnp.zeros((SUB, LANES), f32)
         for k in range(SUB):
             xs = [row(x_ref, base + k, h) for h in range(HALVES)]
             us = [row(u_ref, base + k, h) for h in range(HALVES)]
@@ -281,7 +304,6 @@
     start = (zero(), zero(), zero(), zero(), zero())
     state, moment, plain, first, second = lax.fori_loop(0, BLOCKS, block, start)
 
-    sub = lax.broadcasted_iota(jnp.int32, (SUB, LANES), 0)
 
     def inside(i, carry):
         sums, gains = carry
@@ -291,15 +313,15 @@
             at = span(base, SUB, h)
             x = x_ref[at]
             new_gains.append(gains[h] + u_ref[at] * local_ref[at])
-            later = g_ref[at]
-            own = [sums[h][0] + x * later]
-            for d in range(1, SUB):
-                moved = jnp.where(sub < SUB - d, pltpu.roll(later, SUB - d, 0), 0.0)
-                own.append(sums[h][d] + x * moved)
+            wider = pl.multiple_of((h * BLOCKS + i) * 2 * SUB, 2 * SUB)
+            own = [
+                sums[h][d] + x * padded_ref[pl.ds(wider + d, SUB), :] for d in range(SUB)
+            ]
             new_sums.append(own)
         return new_sums, new_gains
 
     fetch.wait()
+    fetch_g.wait()
     none = jnp.zeros((SUB, LANES), f32)
     sums, gains = lax.fori_loop(
         0, BLOCKS, inside, ([[none] * SUB for _ in range(HALVES)], [none] * HALVES), unroll=2
@@ -323,11 +345,8 @@
             for h in range(HALVES):
                 at = g * SUB * HALVES * SUB + h * SUB + q
                 flat_ref[pl.ds(at, SUB, stride=HALVES * SUB), :] = sent[q][g][h]
-    copy = pltpu.make_async_copy(send_ref, send_out, done.at[4])
-    copy.start()
     for store in stores:
         store.wait()
-    copy.wait()
 
 
 def shifted(value, k):
@@ -388,18 +407,18 @@
     ]
 
 
-def correct_kernel(
+def fill_totals(
     recv_ref,
     local_ref,
-    full_ref,
+    log_rate_ref,
+    residue_ref,
+    total_ref,
+    into_ref,
     fade_ref,
-    log_rate_ref,
-    send_ref,
-    total_out,
-    into_ref,
-    total_ref,
-    done,
+    rate_ref,
+    weight_ref,
 ):
+    fill_fade(log_rate_ref, residue_ref, fade_ref, rate_ref, weight_ref)
     into = received(recv_ref, 1)
     step = each(lambda v: jnp.exp(jnp.exp(v) * (-float(SPAN))), tiles(log_rate_ref))
     spans = ROWS // SPAN
@@ -408,16 +427,19 @@
             for h in range(HALVES):
                 into_ref[tile_rows(b * MODES * HALVES, g, h), :] = into[g][h]
         into = each(lambda l, v: l * v, step, into)
+    places = [
+        [(g * HALVES + h) * SUB + m for g in range(GROUPS) for m in range(SUB)]
+        for h in range(HALVES)
+    ]
 
     def block(b, carry):
         for h in range(HALVES):
-            places = [(g * HALVES + h) * SUB + m for g in range(GROUPS) for m in range(SUB)]
-            rows = [into_ref[pl.ds(b * MODES * HALVES + at, SUB, stride=0), :] for at in places]
+            rows = [into_ref[pl.ds(b * MODES * HALVES + at, SUB, stride=0), :] for at in places[h]]
             for k in range(SPAN // SUB):
                 own = span(pl.multiple_of(b * SPAN + k * SUB, SUB), SUB, h)
                 terms = [
                     fade_ref[pl.ds(at * SPAN + k * SUB, SUB), :] * rows[m]
-                    for m, at in enumerate(places)
+                    for m, at in enumerate(places[h])
                 ]
                 while len(terms) > 1:
                     terms = [a + b for a, b in zip(terms[::2], terms[1::2])]
@@ -425,18 +447,44 @@
         return carry
 
     lax.fori_loop(0, spans, block, 0)
-    copy = pltpu.make_async_copy(total_ref, total_out, done)
-    copy.start()
-    products = [total_ref[span(0, ROWS, h)] * full_ref[span(0, ROWS, h)] for h in range(HALVES)]
-    send_rows(send_ref, sum(products))
-    copy.wait()
+
+
+def correct_kernel(
+    recv_ref,
+    local_ref,
+    full_ref,
+    log_rate_ref,
+    residue_ref,
+    send_ref,
+    total_ref,
+    into_ref,
+    fade_ref,
+    rate_ref,
+    weight_ref,
+):
+    fill_totals(
+        recv_ref,
+        local_ref,
+        log_rate_ref,
+        residue_ref,
+        total_ref,
+        into_ref,
+        fade_ref,
+        rate_ref,
+        weight_ref,
+    )
+    parts = []
+    for k in range(QUARTERS):
+        own = [span(k * LANES, LANES, h) for h in range(HALVES)]
+        parts.append(lane_totals(sum(total_ref[at] * full_ref[at] for at in own)))
+    send_rows(send_ref, parts)
 
 
 def forward_kernel(
     recv_ref,
     signal_ref,
     inv_ref,
-    total_ref,
+    local_ref,
     stream_ref,
     key_ref,
     query_ref,
@@ -454,7 +502,23 @@
     grad_gain_ref,
     conv_ref,
     x_ref,
+    total_ref,
+    into_ref,
+    fade_ref,
+    rate_ref,
+    weight_ref,
 ):
+    fill_totals(
+        recv_ref,
+        local_ref,
+        log_rate_ref,
+        residue_ref,
+        total_ref,
+        into_ref,
+        fade_ref,
+        rate_ref,
+        weight_ref,
+    )
     x_ref[...] = signal_ref[...].astype(f32)
     lam = each(lambda v: jnp.exp(-jnp.exp(v)), tiles(log_rate_ref))
     res = tiles(residue_ref)
@@ -502,7 +566,7 @@
 
 def finish_kernel(recv_ref, left_ref, right_ref, grad_stream_ref):
     inner = columns(jnp.sum(recv_ref[...], axis=0) / D)
-    for k in range(4):
+    for k in range(QUARTERS):
         part = pl.ds(k * LANES, LANES)
         across = jnp.broadcast_to(inner[k], (LANES, LANES))
         for h in range(HALVES):
@@ -532,37 +596,56 @@
     log_rate_own = lax.dynamic_slice_in_dim(log_rate_t.reshape(CHUNKS, LANES), me, 1, 0)
     residue_own = lax.dynamic_slice_in_dim(residue_t.reshape(CHUNKS, LANES), me, 1, 0)
     table = (BLOCKS * MODES * HALVES, LANES)
-    few = (MODES * HALVES, LANES)
     packed = (CHUNKS, SUB, LANES)
-    grad_conv, local_grad, p, w, across, across_lag, gain = call(
+    own = (1, LANES)
+    (
+        grad_conv,
+        local_grad,
+        p,
+        w,
+        across,
+        across_lag,
+        gain,
+        log_rate_own,
+        residue_own,
+    ) = call(
         adjoint_kernel,
-        "vvvvv",
+        "v" * 7,
         [
-            (split, f32, "v"),
+            ((HALVES * BLOCKS, SUB, LANES), f32, "a"),
             (split, f32, "a"),
             (modes, f32, "v"),
             (modes, f32, "v"),
             (table, f32, "v"),
             (table, f32, "v"),
             ((1, COLS), f32, "v"),
+            (own, f32, "v"),
+            (own, f32, "v"),
         ],
-        [pltpu.VMEM(split, f32), pltpu.SemaphoreType.DMA],
+        [pltpu.VMEM(split, f32), pltpu.VMEM(split, f32), pltpu.SemaphoreType.DMA((2,))],
         name="adjoint",
-    )(query_gate, grad_output, log_rate_t, residue_t, norm_gain[None, :])
+    )(
+        query_gate,
+        grad_output,
+        log_rate_t,
+        residue_t,
+        norm_gain[None, :],
+        log_rate_own,
+        residue_own,
+    )
     rows = (ROWS, LANES)
     sent, signal, inv, full = call(
         state_kernel,
-        "vvvvvavvvvv",
-        [(packed, f32, "a"), (split, bf16, "a"), (rows, f32, "a"), (split, f32, "a")],
+        "vvvvaavvvvv",
+        [(packed, f32, "v"), (split, bf16, "a"), (rows, f32, "a"), (split, f32, "v")],
         [
-            pltpu.VMEM(packed, f32),
             pltpu.VMEM(split, bf16),
             pltpu.VMEM(rows, f32),
             pltpu.VMEM(split, f32),
             pltpu.VMEM(split, f32),
             pltpu.VMEM(split, f32),
-            pltpu.VMEM(split, f32),
-            pltpu.SemaphoreType.DMA((5,)),
+            pltpu.VMEM((2 * HALVES * ROWS, LANES), f32),
+            pltpu.SemaphoreType.DMA((4,)),
         ],
         name="state",
     )(
@@ -570,7 +653,7 @@
         stream,
         key_gate,
         gain,
-        grad_conv,
+        in_hbm(grad_conv),
         in_hbm(local_grad),
         p,
         w,
@@ -579,28 +662,20 @@
         log_rate_t,
     )
     got = exchange(sent, "ctx")
-    (fade,) = call(
-        fade_kernel,
-        "vva",
-        [((MODES * HALVES * SPAN, LANES), f32, "v")],
-        [pltpu.VMEM(few, f32), pltpu.VMEM(few, f32)],
-        name="fade",
-    )(log_rate_t, residue_t, in_hbm(inv))
     (sent,) = call(owner_kernel, "vvv", [(packed, f32, "v")], name="owner")(
         got, log_rate_own, residue_own
     )
     got = exchange(sent, "ctx")
-    inner, total = call(
-        correct_kernel,
-        "vvvvv",
-        [(tile, f32, "v"), (split, f32, "a")],
-        [
-            pltpu.VMEM((ROWS // SPAN * MODES * HALVES, LANES), f32),
-            pltpu.VMEM(split, f32),
-            pltpu.SemaphoreType.DMA,
-        ],
-        name="correct",
-    )(got, local_grad, full, fade, log_rate_t)
+    totals = [
+        pltpu.VMEM(split, f32),
+        pltpu.VMEM((ROWS // SPAN * MODES * HALVES, LANES), f32),
+        pltpu.VMEM((MODES * HALVES * SPAN, LANES), f32),
+        pltpu.VMEM((MODES * HALVES, LANES), f32),
+        pltpu.VMEM((MODES * HALVES, LANES), f32),
+    ]
+    (inner,) = call(correct_kernel, "vvvvv", [(tile, f32, "v")], totals, name="correct")(
+        got, local_grad, full, log_rate_t, residue_t
+    )
     inner = exchange(inner, "ch")
     output, grad_key, grad_query, left, right, grad_residue, grad_rate, grad_gain = call(
         forward_kernel,
@@ -615,13 +690,13 @@
             (modes, f32, "v"),
             ((1, COLS), f32, "v"),
         ],
-        [pltpu.VMEM(split, f32), pltpu.VMEM(split, f32)],
+        [pltpu.VMEM(split, f32), pltpu.VMEM(split, f32), *totals],
         name="forward",
     )(
         got,
         signal,
         inv,
-        total,
+        local_grad,
         stream,
         key_gate,
         query_gate,
@@ -630,7 +705,9 @@
         log_rate_t,
         residue_t,
     )
-    (grad_stream,) = call(finish_kernel, "vvv", [(wide, bf16, "v")], name="finish")(inner, left, right)
+    (grad_stream,) = call(finish_kernel, "vvv", [(wide, bf16, "v")], name="finish")(
+        inner, left, right
+    )
     return (
         output,
         grad_stream,

time: 83.4 us -> 82.1 us (0.984)
  blocking collectives: 0 us -> 28 us
  waiting for transfers between devices: 28.4 us -> 12.1 us
  starting transfers between devices: 33.9 us -> 21.7 us
  Pallas kernels: 16.2 us -> 15 us
    all_to_all x0 -> x2, blocking collectives: none -> 28 us  [exchange(): return lax.all_to_all(value, axis, split_axis=0, concat_axis=0, tiled=True)]
    all_to_all x4 -> x2, waiting for transfers between devices: 28.4 us -> 12.1 us  [exchange(): return lax.all_to_all(value, axis, split_axis=0, concat_axis=0, tiled=True)]
    all_to_all x4 -> x2, starting transfers between devices: 33.9 us -> 21.7 us  [exchange(): return lax.all_to_all(value, axis, split_axis=0, concat_axis=0, tiled=True)]
    pallas_call x4 -> x3, Pallas kernels: 10.6 us -> 9.09 us  [the longest x1 4.01 us: local(): call(adjoint_kernel, 'v' * 7, [((HALVES * BLOCKS, SUB, LANES), f32, 'a'),...]
    unnamed x28 -> x26, local copies, waits for them, and re-layouts: 3.61 us -> 2.35 us
    pallas_call x1, Pallas kernels: 3.09 us -> 4.05 us  [local(): call(forward_kernel, 'v' * 11, [(wide, bf16, 'v'), (wide, bf16, 'v'), (wi...]
  transfers between devices with their start and end apart: 4 -> 2, of which waited for: 4 -> 2; matrix products, arithmetic and copies ran while one was open for 0% -> 2% of each run, Pallas kernels for 9% -> 10%
where the time goes in v4:
time: 82.1 us; the launch traced here: 81.4 us
  blocking collectives  28 us (34%)
  starting transfers between devices  21.7 us (26%)
  Pallas kernels  15 us (18%)
  waiting for transfers between devices  12.1 us (15%)
  local copies, waits for them, and re-layouts  3.87 us (5%)
    all_to_all x2, blocking collectives, exchange(): return lax.all_to_all(value, axis, split_axis=0, concat_axis=0, tiled=True)  28 us
    all_to_all x2, starting transfers between devices, exchange(): return lax.all_to_all(value, axis, split_axis=0, concat_axis=0, tiled=True)  21.7 us
    all_to_all x2, waiting for transfers between devices, exchange(): return lax.all_to_all(value, axis, split_axis=0, concat_axis=0, tiled=True)  12.1 us
    pallas_call x1, Pallas kernels, local(): call(forward_kernel, 'v' * 11, [(wide, bf16, 'v'), (wide, bf16, 'v'), (wi...  4.05 us
    pallas_call x1, Pallas kernels, local(): call(adjoint_kernel, 'v' * 7, [((HALVES * BLOCKS, SUB, LANES), f32, 'a'),...  4.01 us
    pallas_call x1, Pallas kernels, local(): call(state_kernel, 'vvvvaavvvvv', [(packed, f32, 'v'), (split, bf16, 'a')...  3.34 us
    unnamed x26, local copies, waits for them, and re-layouts  2.35 us
    pallas_call x1, Pallas kernels, local(): call(correct_kernel, 'vvvvv', [(tile, f32, 'v')], totals, name='correct')  1.73 us
  transfers between devices with their start and end apart: 2, of which 2 were waited for; matrix products, arithmetic and copies ran while one was open for 2% of the time, Pallas kernels for 10%

profile of v4, /device:TPU:1, one launch (start us, length us, event | category | flops | bytes accessed | tf_op | source)
XLA Modules:
  0.0 81.4 jit_solution(8518383848066984954)
XLA Ops:
  0.6 0.0 copy-start.1
  0.6 0.9 %copy-done.1 = bf16[512,256]{1,0:T(8,128)(2,1)S(1)} copy-done((bf16[512,256]{1,0:T(8,128)(2,1)S(1)}, bf16[512,256]{1,0:T(8,128)(2,1)}, u32[]{:S(2)}) %copy-start.1) | copy-done | bytes 262168
  1.6 0.8 square.1
  2.4 15.7 %all-to-all-start = ((f32[16,8,128]{2,1,0:T(8,128)}), f32[16,8,128]{2,1,0:T(8,128)S(1)}, u32[]{:S(2)}, u32[]{:S(2)}) async-start(f32[16,8,128]{2,1,0:T(8,128)} %square.1), calls=%async_computation | async-start | bytes 131072 | tf_op jit(solution)/shard_map/all_to_all | solution.py:583
  18.1 0.7 reshape.21
  18.8 0.8 reshape.20
  19.6 0.0 copy-done.4
  19.7 0.0 copy-done.5
  19.7 0.0 copy-done.7
  19.7 0.6 copy-done.12
  20.3 0.7 copy-done.8
  21.0 4.0 %adjoint.1 = (f32[128,8,128]{2,1,0:T(8,128)}, f32[1024,128]{1,0:T(8,128)}, f32[16,256]{1,0:T(8,128)S(1)}, f32[16,256]{1,0:T(8,128)S(1)}, f32[2048,128]{1,0:T(8,1...) custom-call(bf16[512,256]{1,0:T(8,128)(2,1)S(1)} %copy-done.4, ...), custom_call_target="tpu_custom_call" | custom-call | flops 4194304 | bytes 2097152 | tf_op jit(solution)/shard_map/adjoint/pallas_call | solution.py:611
  25.1 4.6 %all-to-all-done.recv_ref = f32[16,8,128]{2,1,0:T(8,128)S(1)} async-done(((f32[16,8,128]{2,1,0:T(8,128)}), f32[16,8,128]{2,1,0:T(8,128)S(1)}, u32[]{:S(2)}, u32[]{:S(2)}) %all-to-all-start) | async-done | bytes 65568 | tf_op jit(solution)/shard_map/all_to_all | solution.py:583
  29.7 0.0 copy-done.2
  29.7 0.0 copy-done.3
  29.7 3.3 %state.1 = (f32[32,8,128]{2,1,0:T(8,128)S(1)}, bf16[1024,128]{1,0:T(8,128)(2,1)}, f32[512,128]{1,0:T(8,128)}, f32[1024,128]{1,0:T(8,128)S(1)}) custom-call(f32[16,8,128]{2,1,0:T(8,128)S(1)} %all-to-all-done.recv_ref, bf16[512,256]{1,0:T(8,128)(2,1)S(1)} %copy-done.2, bf16[512,256]{1,0:T(8,128)(2,1)S(1)} %copy-done.3, ...), custom_call_target="tpu_custom_call" | custom-call | flops 4194304 | bytes 2097152 | tf_op jit(solution)/shard_map/state/pallas_call | solution.py:637
  33.0 0.0 copy-start
  33.0 16.7 %all_to_all.20.recv_ref = f32[32,8,128]{2,1,0:T(8,128)S(1)} all-to-all(f32[32,8,128]{2,1,0:T(8,128)S(1)} %get-tuple-element.35), channel_id=1, replica_groups=mesh['ctx'=32,'ch'=16] {'ctx'}, dimensions={0} | all-to-all | bytes 262144 | tf_op jit(solution)/shard_map/all_to_all | solution.py:583
  49.8 0.1 owner.1
  49.9 0.0 copy-start.9
  49.9 11.2 %all_to_all.21.recv_ref = f32[32,8,128]{2,1,0:T(8,128)S(1)} all-to-all(f32[32,8,128]{2,1,0:T(8,128)S(1)} %owner.1), channel_id=1, replica_groups=mesh['ctx'=32,'ch'=16] {'ctx'}, dimensions={0} | all-to-all | bytes 262144 | tf_op jit(solution)/shard_map/all_to_all | solution.py:583
  61.1 0.0 copy-done
  61.1 0.0 copy-done.9
  61.1 0.0 copy-start.11
  61.2 1.7 %correct.1 = f32[16,8,128]{2,1,0:T(8,128)} custom-call(f32[32,8,128]{2,1,0:T(8,128)S(1)} %all_to_all.21.recv_ref, f32[1024,128]{1,0:T(8,128)S(1)} %copy-done, f32[1024,128]{1,0:T(8,128)S(1)} %get-tuple-element.41.full_ref, f32[16,256]{1,0:T(8,128)S(1)} %bitcast.9, f32[16,256]{1,0:T(8,128)S(1)} %bitcast.13), custom_call_target="tpu_custom_call" | custom-call | flops 4194304 | bytes 2097152 | tf_op jit(solution)/shard_map/correct/pallas_call | solution.py:676
  62.9 6.0 %all-to-all-start.3 = ((f32[16,8,128]{2,1,0:T(8,128)}), f32[16,8,128]{2,1,0:T(8,128)S(1)}, u32[]{:S(2)}, u32[]{:S(2)}) async-start(f32[16,8,128]{2,1,0:T(8,128)} %correct.1), calls=%async_computation.3 | async-start | bytes 131072 | tf_op jit(solution)/shard_map/all_to_all | solution.py:583
  68.9 0.0 copy-done.6
  68.9 0.0 copy-done.10
  68.9 0.0 copy-done.11
  68.9 4.0 %forward.1 = (bf16[512,256]{1,0:T(8,128)(2,1)}, bf16[512,256]{1,0:T(8,128)(2,1)}, bf16[512,256]{1,0:T(8,128)(2,1)}, f32[1024,128]{1,0:T(8,128)S(1)}, f32[1024,12...) custom-call(f32[32,8,128]{2,1,0:T(8,128)S(1)} %all_to_all.21.recv_ref, ...), custom_call_target="tpu_custom_call" | custom-call | flops 4194304 | bytes 2097152 | tf_op jit(solution)/shard_map/forward/pallas_call | solution.py:680
  73.0 7.5 %all-to-all-done.3.recv_ref = f32[16,8,128]{2,1,0:T(8,128)S(1)} async-done(((f32[16,8,128]{2,1,0:T(8,128)}), f32[16,8,128]{2,1,0:T(8,128)S(1)}, u32[]{:S(2)}, u32[]{:S(2)}) %all-to-all-start.3) | async-done | bytes 65568 | tf_op jit(solution)/shard_map/all_to_all | solution.py:583
  80.5 1.0 %finish.1 = bf16[512,256]{1,0:T(8,128)(2,1)} custom-call(f32[16,8,128]{2,1,0:T(8,128)S(1)} %all-to-all-done.3.recv_ref, f32[1024,128]{1,0:T(8,128)S(1)} %get-tuple-element.42.left_ref, f32[1024,128]{1,0:T(8,128)S(1)} %get-tuple-element.43.right_ref), custom_call_target="tpu_custom_call" | custom-call | flops 4194304 | bytes 2097152 | tf_op jit(solution)/shard_map/finish/pallas_call | solution.py:708
  (10 shorter events, 0.0 us)
Async XLA Ops:
  0.6 1.0 %copy-start.1 = (bf16[512,256]{1,0:T(8,128)(2,1)S(1)}, bf16[512,256]{1,0:T(8,128)(2,1)}, u32[]{:S(2)}) copy-start(bf16[512,256]{1,0:T(8,128)(2,1)} %stream_ref.5) | copy-start | bytes 786436
  1.6 18.1 %copy-start.4 = (bf16[512,256]{1,0:T(8,128)(2,1)S(1)}, bf16[512,256]{1,0:T(8,128)(2,1)}, u32[]{:S(2)}) copy-start(bf16[512,256]{1,0:T(8,128)(2,1)} %query_ref.3) | copy-start | bytes 786436
  1.6 18.1 %copy-start.5 = (bf16[512,256]{1,0:T(8,128)(2,1)S(1)}, bf16[512,256]{1,0:T(8,128)(2,1)}, u32[]{:S(2)}) copy-start(bf16[512,256]{1,0:T(8,128)(2,1)} %grad_ref.3) | copy-start | bytes 786436
  2.4 27.3 %all-to-all-start = ((f32[16,8,128]{2,1,0:T(8,128)}), f32[16,8,128]{2,1,0:T(8,128)S(1)}, u32[]{:S(2)}, u32[]{:S(2)}) async-start(f32[16,8,128]{2,1,0:T(8,128)} %square.1), calls=%async_computation | async-start | bytes 131072 | tf_op jit(solution)/shard_map/all_to_all | solution.py:583
  18.8 0.8 %copy-start.7 = (f32[256,16]{0,1:T(8,128)S(1)}, f32[256,16]{0,1:T(8,128)}, u32[]{:S(2)}) copy-start(f32[256,16]{0,1:T(8,128)} %param.13) | copy-start | bytes 49156
  19.6 0.7 copy-start.12
  20.3 0.7 copy-start.8
  21.0 8.6 %copy-start.2 = (bf16[512,256]{1,0:T(8,128)(2,1)S(1)}, bf16[512,256]{1,0:T(8,128)(2,1)}, u32[]{:S(2)}) copy-start(bf16[512,256]{1,0:T(8,128)(2,1)} %stream_ref.5) | copy-start | bytes 786436
  21.0 8.6 %copy-start.3 = (bf16[512,256]{1,0:T(8,128)(2,1)S(1)}, bf16[512,256]{1,0:T(8,128)(2,1)}, u32[]{:S(2)}) copy-start(bf16[512,256]{1,0:T(8,128)(2,1)} %key_ref.3) | copy-start | bytes 786436
  33.0 28.1 %copy-start = (f32[1024,128]{1,0:T(8,128)S(1)}, f32[1024,128]{1,0:T(8,128)}, u32[]{:S(2)}) copy-start(f32[1024,128]{1,0:T(8,128)} %get-tuple-element.30.local_in.local_ref) | copy-start | bytes 1572868
  49.9 11.3 %copy-start.9 = (f32[256,16]{0,1:T(8,128)S(1)}, f32[256,16]{0,1:T(8,128)}, u32[]{:S(2)}) copy-start(f32[256,16]{0,1:T(8,128)} %param.12) | copy-start | bytes 49156
  61.1 7.8 %copy-start.6 = (bf16[512,256]{1,0:T(8,128)(2,1)S(1)}, bf16[512,256]{1,0:T(8,128)(2,1)}, u32[]{:S(2)}) copy-start(bf16[512,256]{1,0:T(8,128)(2,1)} %grad_ref.3) | copy-start | bytes 786436
  61.1 7.8 %copy-start.10 = (bf16[1024,128]{1,0:T(8,128)(2,1)S(1)}, bf16[1024,128]{1,0:T(8,128)(2,1)}, u32[]{:S(2)}) copy-start(bf16[1024,128]{1,0:T(8,128)(2,1)} %get-tuple-element.38.signal_ref) | copy-start | bytes 786436
  61.1 7.8 %copy-start.11 = (f32[512,128]{1,0:T(8,128)S(1)}, f32[512,128]{1,0:T(8,128)}, u32[]{:S(2)}) copy-start(f32[512,128]{1,0:T(8,128)} %get-tuple-element.39.inv_ref) | copy-start | bytes 786436
  62.9 17.6 %all-to-all-start.3 = ((f32[16,8,128]{2,1,0:T(8,128)}), f32[16,8,128]{2,1,0:T(8,128)S(1)}, u32[]{:S(2)}, u32[]{:S(2)}) async-start(f32[16,8,128]{2,1,0:T(8,128)} %correct.1), calls=%async_computation.3 | async-start | bytes 131072 | tf_op jit(solution)/shard_map/all_to_all | solution.py:583

commit v5 on v4

--- a/solution.py
+++ b/solution.py
@@ -302,7 +302,7 @@
 
     zero = zeros_tiles
     start = (zero(), zero(), zero(), zero(), zero())
-    state, moment, plain, first, second = lax.fori_loop(0, BLOCKS, block, start)
+    state, moment, plain, first, second = lax.fori_loop(0, BLOCKS, block, start, unroll=4)
 
 
     def inside(i, carry):
@@ -324,7 +324,7 @@
     fetch_g.wait()
     none = jnp.zeros((SUB, LANES), f32)
     sums, gains = lax.fori_loop(
-        0, BLOCKS, inside, ([[none] * SUB for _ in range(HALVES)], [none] * HALVES), unroll=2
+        0, BLOCKS, inside, ([[none] * SUB for _ in range(HALVES)], [none] * HALVES), unroll=8
     )
     near, near_lag = zero(), zero()
     for d in reversed(range(SUB)):
@@ -446,7 +446,7 @@
                 total_ref[own] = local_ref[own] + terms[0]
         return carry
 
-    lax.fori_loop(0, spans, block, 0)
+    lax.fori_loop(0, spans, block, 0, unroll=4)
 
 
 def correct_kernel(

time: 82.1 us -> 81.3 us (level)
  Pallas kernels: 15 us -> 14 us
where the time goes in v5:
time: 81.3 us; the launch traced here: 80.7 us
  blocking collectives  28 us (34%)
  starting transfers between devices  21.7 us (27%)
  Pallas kernels  14 us (17%)
  waiting for transfers between devices  12.3 us (15%)
  local copies, waits for them, and re-layouts  3.87 us (5%)
    all_to_all x2, blocking collectives, exchange(): return lax.all_to_all(value, axis, split_axis=0, concat_axis=0, tiled=True)  28 us
    all_to_all x2, starting transfers between devices, exchange(): return lax.all_to_all(value, axis, split_axis=0, concat_axis=0, tiled=True)  21.7 us
    all_to_all x2, waiting for transfers between devices, exchange(): return lax.all_to_all(value, axis, split_axis=0, concat_axis=0, tiled=True)  12.3 us
    pallas_call x1, Pallas kernels, local(): call(adjoint_kernel, 'v' * 7, [((HALVES * BLOCKS, SUB, LANES), f32, 'a'),...  4.01 us
    pallas_call x1, Pallas kernels, local(): call(forward_kernel, 'v' * 11, [(wide, bf16, 'v'), (wide, bf16, 'v'), (wi...  3.83 us
    pallas_call x1, Pallas kernels, local(): call(state_kernel, 'vvvvaavvvvv', [(packed, f32, 'v'), (split, bf16, 'a')...  2.76 us
    unnamed x26, local copies, waits for them, and re-layouts  2.35 us
  transfers between devices with their start and end apart: 2, of which 2 were waited for; matrix products, arithmetic and copies ran while one was open for 2% of the time, Pallas kernels for 10%

profile of v5, /device:TPU:1, one launch (start us, length us, event | category | flops | bytes accessed | tf_op | source)
XLA Modules:
  0.0 80.7 jit_solution(7732189066204721505)
XLA Ops:
  0.6 0.0 copy-start.1
  0.6 0.9 %copy-done.1 = bf16[512,256]{1,0:T(8,128)(2,1)S(1)} copy-done((bf16[512,256]{1,0:T(8,128)(2,1)S(1)}, bf16[512,256]{1,0:T(8,128)(2,1)}, u32[]{:S(2)}) %copy-start.1) | copy-done | bytes 262168
  1.6 0.8 square.1
  2.4 15.7 %all-to-all-start = ((f32[16,8,128]{2,1,0:T(8,128)}), f32[16,8,128]{2,1,0:T(8,128)S(1)}, u32[]{:S(2)}, u32[]{:S(2)}) async-start(f32[16,8,128]{2,1,0:T(8,128)} %square.1), calls=%async_computation | async-start | bytes 131072 | tf_op jit(solution)/shard_map/all_to_all | solution.py:583
  18.1 0.7 reshape.21
  18.8 0.8 reshape.20
  19.6 0.0 copy-done.4
  19.7 0.0 copy-done.5
  19.7 0.0 copy-done.7
  19.7 0.6 copy-done.12
  20.3 0.7 copy-done.8
  21.0 4.0 %adjoint.1 = (f32[128,8,128]{2,1,0:T(8,128)}, f32[1024,128]{1,0:T(8,128)}, f32[16,256]{1,0:T(8,128)S(1)}, f32[16,256]{1,0:T(8,128)S(1)}, f32[2048,128]{1,0:T(8,1...) custom-call(bf16[512,256]{1,0:T(8,128)(2,1)S(1)} %copy-done.4, ...), custom_call_target="tpu_custom_call" | custom-call | flops 4194304 | bytes 2097152 | tf_op jit(solution)/shard_map/adjoint/pallas_call | solution.py:611
  25.1 4.6 %all-to-all-done.recv_ref = f32[16,8,128]{2,1,0:T(8,128)S(1)} async-done(((f32[16,8,128]{2,1,0:T(8,128)}), f32[16,8,128]{2,1,0:T(8,128)S(1)}, u32[]{:S(2)}, u32[]{:S(2)}) %all-to-all-start) | async-done | bytes 65568 | tf_op jit(solution)/shard_map/all_to_all | solution.py:583
  29.7 0.0 copy-done.2
  29.7 0.0 copy-done.3
  29.7 2.8 %state.1 = (f32[32,8,128]{2,1,0:T(8,128)S(1)}, bf16[1024,128]{1,0:T(8,128)(2,1)}, f32[512,128]{1,0:T(8,128)}, f32[1024,128]{1,0:T(8,128)S(1)}) custom-call(f32[16,8,128]{2,1,0:T(8,128)S(1)} %all-to-all-done.recv_ref, bf16[512,256]{1,0:T(8,128)(2,1)S(1)} %copy-done.2, bf16[512,256]{1,0:T(8,128)(2,1)S(1)} %copy-done.3, ...), custom_call_target="tpu_custom_call" | custom-call | flops 4194304 | bytes 2097152 | tf_op jit(solution)/shard_map/state/pallas_call | solution.py:637
  32.4 0.0 copy-start
  32.5 16.7 %all_to_all.20.recv_ref = f32[32,8,128]{2,1,0:T(8,128)S(1)} all-to-all(f32[32,8,128]{2,1,0:T(8,128)S(1)} %get-tuple-element.35), channel_id=1, replica_groups=mesh['ctx'=32,'ch'=16] {'ctx'}, dimensions={0} | all-to-all | bytes 262144 | tf_op jit(solution)/shard_map/all_to_all | solution.py:583
  49.2 0.1 owner.1
  49.3 0.0 copy-start.9
  49.3 11.2 %all_to_all.21.recv_ref = f32[32,8,128]{2,1,0:T(8,128)S(1)} all-to-all(f32[32,8,128]{2,1,0:T(8,128)S(1)} %owner.1), channel_id=1, replica_groups=mesh['ctx'=32,'ch'=16] {'ctx'}, dimensions={0} | all-to-all | bytes 262144 | tf_op jit(solution)/shard_map/all_to_all | solution.py:583
  60.5 0.0 copy-done
  60.5 0.0 copy-done.9
  60.6 0.0 copy-start.11
  60.6 1.5 %correct.1 = f32[16,8,128]{2,1,0:T(8,128)} custom-call(f32[32,8,128]{2,1,0:T(8,128)S(1)} %all_to_all.21.recv_ref, f32[1024,128]{1,0:T(8,128)S(1)} %copy-done, f32[1024,128]{1,0:T(8,128)S(1)} %get-tuple-element.41.full_ref, f32[16,256]{1,0:T(8,128)S(1)} %bitcast.9, f32[16,256]{1,0:T(8,128)S(1)} %bitcast.13), custom_call_target="tpu_custom_call" | custom-call | flops 4194304 | bytes 2097152 | tf_op jit(solution)/shard_map/correct/pallas_call | solution.py:676
  62.1 6.0 %all-to-all-start.3 = ((f32[16,8,128]{2,1,0:T(8,128)}), f32[16,8,128]{2,1,0:T(8,128)S(1)}, u32[]{:S(2)}, u32[]{:S(2)}) async-start(f32[16,8,128]{2,1,0:T(8,128)} %correct.1), calls=%async_computation.3 | async-start | bytes 131072 | tf_op jit(solution)/shard_map/all_to_all | solution.py:583
  68.1 0.0 copy-done.6
  68.1 0.0 copy-done.10
  68.1 0.0 copy-done.11
  68.1 3.8 %forward.1 = (bf16[512,256]{1,0:T(8,128)(2,1)}, bf16[512,256]{1,0:T(8,128)(2,1)}, bf16[512,256]{1,0:T(8,128)(2,1)}, f32[1024,128]{1,0:T(8,128)S(1)}, f32[1024,12...) custom-call(f32[32,8,128]{2,1,0:T(8,128)S(1)} %all_to_all.21.recv_ref, ...), custom_call_target="tpu_custom_call" | custom-call | flops 4194304 | bytes 2097152 | tf_op jit(solution)/shard_map/forward/pallas_call | solution.py:680
  72.0 7.7 %all-to-all-done.3.recv_ref = f32[16,8,128]{2,1,0:T(8,128)S(1)} async-done(((f32[16,8,128]{2,1,0:T(8,128)}), f32[16,8,128]{2,1,0:T(8,128)S(1)}, u32[]{:S(2)}, u32[]{:S(2)}) %all-to-all-start.3) | async-done | bytes 65568 | tf_op jit(solution)/shard_map/all_to_all | solution.py:583
  79.7 1.0 %finish.1 = bf16[512,256]{1,0:T(8,128)(2,1)} custom-call(f32[16,8,128]{2,1,0:T(8,128)S(1)} %all-to-all-done.3.recv_ref, f32[1024,128]{1,0:T(8,128)S(1)} %get-tuple-element.42.left_ref, f32[1024,128]{1,0:T(8,128)S(1)} %get-tuple-element.43.right_ref), custom_call_target="tpu_custom_call" | custom-call | flops 4194304 | bytes 2097152 | tf_op jit(solution)/shard_map/finish/pallas_call | solution.py:708
  (10 shorter events, 0.0 us)
Async XLA Ops:
  0.6 1.0 %copy-start.1 = (bf16[512,256]{1,0:T(8,128)(2,1)S(1)}, bf16[512,256]{1,0:T(8,128)(2,1)}, u32[]{:S(2)}) copy-start(bf16[512,256]{1,0:T(8,128)(2,1)} %stream_ref.5) | copy-start | bytes 786436
  1.6 18.1 %copy-start.4 = (bf16[512,256]{1,0:T(8,128)(2,1)S(1)}, bf16[512,256]{1,0:T(8,128)(2,1)}, u32[]{:S(2)}) copy-start(bf16[512,256]{1,0:T(8,128)(2,1)} %query_ref.3) | copy-start | bytes 786436
  1.6 18.1 %copy-start.5 = (bf16[512,256]{1,0:T(8,128)(2,1)S(1)}, bf16[512,256]{1,0:T(8,128)(2,1)}, u32[]{:S(2)}) copy-start(bf16[512,256]{1,0:T(8,128)(2,1)} %grad_ref.3) | copy-start | bytes 786436
  2.4 27.3 %all-to-all-start = ((f32[16,8,128]{2,1,0:T(8,128)}), f32[16,8,128]{2,1,0:T(8,128)S(1)}, u32[]{:S(2)}, u32[]{:S(2)}) async-start(f32[16,8,128]{2,1,0:T(8,128)} %square.1), calls=%async_computation | async-start | bytes 131072 | tf_op jit(solution)/shard_map/all_to_all | solution.py:583
  18.8 0.8 %copy-start.7 = (f32[256,16]{0,1:T(8,128)S(1)}, f32[256,16]{0,1:T(8,128)}, u32[]{:S(2)}) copy-start(f32[256,16]{0,1:T(8,128)} %param.13) | copy-start | bytes 49156
  19.6 0.7 copy-start.12
  20.3 0.7 copy-start.8
  21.0 8.6 %copy-start.2 = (bf16[512,256]{1,0:T(8,128)(2,1)S(1)}, bf16[512,256]{1,0:T(8,128)(2,1)}, u32[]{:S(2)}) copy-start(bf16[512,256]{1,0:T(8,128)(2,1)} %stream_ref.5) | copy-start | bytes 786436
  21.0 8.6 %copy-start.3 = (bf16[512,256]{1,0:T(8,128)(2,1)S(1)}, bf16[512,256]{1,0:T(8,128)(2,1)}, u32[]{:S(2)}) copy-start(bf16[512,256]{1,0:T(8,128)(2,1)} %key_ref.3) | copy-start | bytes 786436
  32.4 28.1 %copy-start = (f32[1024,128]{1,0:T(8,128)S(1)}, f32[1024,128]{1,0:T(8,128)}, u32[]{:S(2)}) copy-start(f32[1024,128]{1,0:T(8,128)} %get-tuple-element.30.local_in.local_ref) | copy-start | bytes 1572868
  49.3 11.3 %copy-start.9 = (f32[256,16]{0,1:T(8,128)S(1)}, f32[256,16]{0,1:T(8,128)}, u32[]{:S(2)}) copy-start(f32[256,16]{0,1:T(8,128)} %param.12) | copy-start | bytes 49156
  60.5 7.5 %copy-start.6 = (bf16[512,256]{1,0:T(8,128)(2,1)S(1)}, bf16[512,256]{1,0:T(8,128)(2,1)}, u32[]{:S(2)}) copy-start(bf16[512,256]{1,0:T(8,128)(2,1)} %grad_ref.3) | copy-start | bytes 786436
  60.6 7.5 %copy-start.10 = (bf16[1024,128]{1,0:T(8,128)(2,1)S(1)}, bf16[1024,128]{1,0:T(8,128)(2,1)}, u32[]{:S(2)}) copy-start(bf16[1024,128]{1,0:T(8,128)(2,1)} %get-tuple-element.38.signal_ref) | copy-start | bytes 786436
  60.6 7.5 %copy-start.11 = (f32[512,128]{1,0:T(8,128)S(1)}, f32[512,128]{1,0:T(8,128)}, u32[]{:S(2)}) copy-start(f32[512,128]{1,0:T(8,128)} %get-tuple-element.39.inv_ref) | copy-start | bytes 786436
  62.1 17.6 %all-to-all-start.3 = ((f32[16,8,128]{2,1,0:T(8,128)}), f32[16,8,128]{2,1,0:T(8,128)S(1)}, u32[]{:S(2)}, u32[]{:S(2)}) async-start(f32[16,8,128]{2,1,0:T(8,128)} %correct.1), calls=%async_computation.3 | async-start | bytes 131072 | tf_op jit(solution)/shard_map/all_to_all | solution.py:583

commit v6 on v5

--- a/solution.py
+++ b/solution.py
@@ -95,11 +95,11 @@
     tile = parts[0]
     for k in range(1, QUARTERS):
         tile = jnp.where(sub == k, parts[k], tile)
-    ref[...] = jnp.broadcast_to(tile[None], (CH, SUB, LANES))
+    ref[...] = jnp.broadcast_to(tile[None, :QUARTERS], (CH, QUARTERS, LANES))
 
 
 def columns(tile):
-    turned = tile.T
+    turned = jnp.concatenate([tile, tile]).T
     return [turned[:, k : k + 1] for k in range(4)]
 
 
@@ -587,7 +587,7 @@
     wide = (ROWS, COLS)
     split = (HALVES * ROWS, LANES)
     modes = (MODES, COLS)
-    tile = (CH, SUB, LANES)
+    tile = (CH, QUARTERS, LANES)
     (squares,) = call(square_kernel, "v", [(tile, f32, "v")], name="square")(stream)
     squares = exchange(squares, "ch")
     log_rate_t = log_rate.T

time: 81.3 us -> 80.5 us (level)
    unnamed x26 -> x24, local copies, waits for them, and re-layouts: 2.35 us -> 3.29 us
  transfers between devices with their start and end apart: 2 -> 2, of which waited for: 2 -> 2; matrix products, arithmetic and copies ran while one was open for 2% -> 0% of each run, Pallas kernels for 10% -> 10%
where the time goes in v6:
time: 80.5 us; the launch traced here: 80.1 us
  blocking collectives  27.9 us (35%)
  starting transfers between devices  21.5 us (27%)
  Pallas kernels  14 us (17%)
  waiting for transfers between devices  12.7 us (16%)
  local copies, waits for them, and re-layouts  3.3 us (4%)
    all_to_all x2, blocking collectives, exchange(): return lax.all_to_all(value, axis, split_axis=0, concat_axis=0, tiled=True)  27.9 us
    all_to_all x2, starting transfers between devices, exchange(): return lax.all_to_all(value, axis, split_axis=0, concat_axis=0, tiled=True)  21.5 us
    all_to_all x2, waiting for transfers between devices, exchange(): return lax.all_to_all(value, axis, split_axis=0, concat_axis=0, tiled=True)  12.7 us
    pallas_call x1, Pallas kernels, local(): call(adjoint_kernel, 'v' * 7, [((HALVES * BLOCKS, SUB, LANES), f32, 'a'),...  4.01 us
    pallas_call x1, Pallas kernels, local(): call(forward_kernel, 'v' * 11, [(wide, bf16, 'v'), (wide, bf16, 'v'), (wi...  3.83 us
    unnamed x24, local copies, waits for them, and re-layouts  3.29 us
    pallas_call x1, Pallas kernels, local(): call(state_kernel, 'vvvvaavvvvv', [(packed, f32, 'v'), (split, bf16, 'a')...  2.76 us
  transfers between devices with their start and end apart: 2, of which 2 were waited for; matrix products, arithmetic and copies ran while one was open for 0% of the time, Pallas kernels for 10%

profile of v6, /device:TPU:1, one launch (start us, length us, event | category | flops | bytes accessed | tf_op | source)
XLA Modules:
  0.0 80.1 jit_solution(17942583848895127454)
XLA Ops:
  0.6 0.0 copy-start.1
  0.6 0.9 %copy-done.1 = bf16[512,256]{1,0:T(8,128)(2,1)S(1)} copy-done((bf16[512,256]{1,0:T(8,128)(2,1)S(1)}, bf16[512,256]{1,0:T(8,128)(2,1)}, u32[]{:S(2)}) %copy-start.1) | copy-done | bytes 262168
  1.6 0.0 copy-start.4
  1.6 0.8 square.1
  2.4 0.0 copy-start.8
  2.4 15.9 %all-to-all-start = ((f32[16,4,128]{2,1,0:T(4,128)}), f32[16,4,128]{2,1,0:T(4,128)S(1)}, u32[]{:S(2)}, u32[]{:S(2)}) async-start(f32[16,4,128]{2,1,0:T(4,128)} %square.1), calls=%async_computation | async-start | bytes 65536 | tf_op jit(solution)/shard_map/all_to_all | solution.py:583
  18.2 0.0 copy-done.8
  18.2 0.0 copy-start.7
  18.3 0.7 copy-done.7
  19.0 0.0 copy-start.11
  19.0 0.0 copy-done.4
  19.0 0.7 copy-done.11
  19.7 0.0 copy-start.5
  19.7 0.9 %copy-done.5 = bf16[512,256]{1,0:T(8,128)(2,1)S(1)} copy-done((bf16[512,256]{1,0:T(8,128)(2,1)S(1)}, bf16[512,256]{1,0:T(8,128)(2,1)}, u32[]{:S(2)}) %copy-start.5) | copy-done | bytes 262168
  20.6 4.0 %adjoint.1 = (f32[128,8,128]{2,1,0:T(8,128)}, f32[1024,128]{1,0:T(8,128)}, f32[16,256]{1,0:T(8,128)S(1)}, f32[16,256]{1,0:T(8,128)S(1)}, f32[2048,128]{1,0:T(8,1...) custom-call(bf16[512,256]{1,0:T(8,128)(2,1)S(1)} %copy-done.4, ...), custom_call_target="tpu_custom_call" | custom-call | flops 4194304 | bytes 2097152 | tf_op jit(solution)/shard_map/adjoint/pallas_call | solution.py:611
  24.6 5.1 %all-to-all-done.recv_ref = f32[16,4,128]{2,1,0:T(4,128)S(1)} async-done(((f32[16,4,128]{2,1,0:T(4,128)}), f32[16,4,128]{2,1,0:T(4,128)S(1)}, u32[]{:S(2)}, u32[]{:S(2)}) %all-to-all-start) | async-done | bytes 32800 | tf_op jit(solution)/shard_map/all_to_all | solution.py:583
  29.7 0.0 copy-done.2
  29.7 0.0 copy-done.3
  29.7 2.8 %state.1 = (f32[32,8,128]{2,1,0:T(8,128)S(1)}, bf16[1024,128]{1,0:T(8,128)(2,1)}, f32[512,128]{1,0:T(8,128)}, f32[1024,128]{1,0:T(8,128)S(1)}) custom-call(f32[16,4,128]{2,1,0:T(4,128)S(1)} %all-to-all-done.recv_ref, bf16[512,256]{1,0:T(8,128)(2,1)S(1)} %copy-done.2, bf16[512,256]{1,0:T(8,128)(2,1)S(1)} %copy-done.3, ...), custom_call_target="tpu_custom_call" | custom-call | flops 4194304 | bytes 2097152 | tf_op jit(solution)/shard_map/state/pallas_call | solution.py:637
  32.5 0.0 copy-start
  32.5 16.7 %all_to_all.20.recv_ref = f32[32,8,128]{2,1,0:T(8,128)S(1)} all-to-all(f32[32,8,128]{2,1,0:T(8,128)S(1)} %get-tuple-element.35), channel_id=1, replica_groups=mesh['ctx'=32,'ch'=16] {'ctx'}, dimensions={0} | all-to-all | bytes 262144 | tf_op jit(solution)/shard_map/all_to_all | solution.py:583
  49.1 0.1 owner.1
  49.2 11.2 %all_to_all.21.recv_ref = f32[32,8,128]{2,1,0:T(8,128)S(1)} all-to-all(f32[32,8,128]{2,1,0:T(8,128)S(1)} %owner.1), channel_id=1, replica_groups=mesh['ctx'=32,'ch'=16] {'ctx'}, dimensions={0} | all-to-all | bytes 262144 | tf_op jit(solution)/shard_map/all_to_all | solution.py:583
  60.5 0.0 copy-done
  60.5 1.5 %correct.1 = f32[16,4,128]{2,1,0:T(4,128)} custom-call(f32[32,8,128]{2,1,0:T(8,128)S(1)} %all_to_all.21.recv_ref, f32[1024,128]{1,0:T(8,128)S(1)} %copy-done, f32[1024,128]{1,0:T(8,128)S(1)} %get-tuple-element.41.full_ref, f32[16,256]{1,0:T(8,128)S(1)} %bitcast.9, f32[16,256]{1,0:T(8,128)S(1)} %bitcast.13), custom_call_target="tpu_custom_call" | custom-call | flops 4194304 | bytes 2097152 | tf_op jit(solution)/shard_map/correct/pallas_call | solution.py:676
  62.0 5.6 %all-to-all-start.3 = ((f32[16,4,128]{2,1,0:T(4,128)}), f32[16,4,128]{2,1,0:T(4,128)S(1)}, u32[]{:S(2)}, u32[]{:S(2)}) async-start(f32[16,4,128]{2,1,0:T(4,128)} %correct.1), calls=%async_computation.3 | async-start | bytes 65536 | tf_op jit(solution)/shard_map/all_to_all | solution.py:583
  67.6 0.0 copy-done.6
  67.6 0.0 copy-done.9
  67.7 0.0 copy-done.10
  67.7 3.8 %forward.1 = (bf16[512,256]{1,0:T(8,128)(2,1)}, bf16[512,256]{1,0:T(8,128)(2,1)}, bf16[512,256]{1,0:T(8,128)(2,1)}, f32[1024,128]{1,0:T(8,128)S(1)}, f32[1024,12...) custom-call(f32[32,8,128]{2,1,0:T(8,128)S(1)} %all_to_all.21.recv_ref, ...), custom_call_target="tpu_custom_call" | custom-call | flops 4194304 | bytes 2097152 | tf_op jit(solution)/shard_map/forward/pallas_call | solution.py:680
  71.5 7.6 %all-to-all-done.3.recv_ref = f32[16,4,128]{2,1,0:T(4,128)S(1)} async-done(((f32[16,4,128]{2,1,0:T(4,128)}), f32[16,4,128]{2,1,0:T(4,128)S(1)}, u32[]{:S(2)}, u32[]{:S(2)}) %all-to-all-start.3) | async-done | bytes 32800 | tf_op jit(solution)/shard_map/all_to_all | solution.py:583
  79.1 1.0 %finish.1 = bf16[512,256]{1,0:T(8,128)(2,1)} custom-call(f32[16,4,128]{2,1,0:T(4,128)S(1)} %all-to-all-done.3.recv_ref, f32[1024,128]{1,0:T(8,128)S(1)} %get-tuple-element.42.left_ref, f32[1024,128]{1,0:T(8,128)S(1)} %get-tuple-element.43.right_ref), custom_call_target="tpu_custom_call" | custom-call | flops 4194304 | bytes 2097152 | tf_op jit(solution)/shard_map/finish/pallas_call | solution.py:708
  (8 shorter events, 0.0 us)
Async XLA Ops:
  0.6 1.0 %copy-start.1 = (bf16[512,256]{1,0:T(8,128)(2,1)S(1)}, bf16[512,256]{1,0:T(8,128)(2,1)}, u32[]{:S(2)}) copy-start(bf16[512,256]{1,0:T(8,128)(2,1)} %stream_ref.5) | copy-start | bytes 786436
  1.6 17.4 %copy-start.4 = (bf16[512,256]{1,0:T(8,128)(2,1)S(1)}, bf16[512,256]{1,0:T(8,128)(2,1)}, u32[]{:S(2)}) copy-start(bf16[512,256]{1,0:T(8,128)(2,1)} %query_ref.3) | copy-start | bytes 786436
  2.4 15.9 %copy-start.8 = (f32[256,16]{0,1:T(8,128)S(1)}, f32[256,16]{0,1:T(8,128)}, u32[]{:S(2)}) copy-start(f32[256,16]{0,1:T(8,128)} %param.12) | copy-start | bytes 49156
  2.4 27.3 %all-to-all-start = ((f32[16,4,128]{2,1,0:T(4,128)}), f32[16,4,128]{2,1,0:T(4,128)S(1)}, u32[]{:S(2)}, u32[]{:S(2)}) async-start(f32[16,4,128]{2,1,0:T(4,128)} %square.1), calls=%async_computation | async-start | bytes 65536 | tf_op jit(solution)/shard_map/all_to_all | solution.py:583
  18.2 0.7 copy-start.7
  19.0 0.7 copy-start.11
  19.7 0.9 %copy-start.5 = (bf16[512,256]{1,0:T(8,128)(2,1)S(1)}, bf16[512,256]{1,0:T(8,128)(2,1)}, u32[]{:S(2)}) copy-start(bf16[512,256]{1,0:T(8,128)(2,1)} %grad_ref.3) | copy-start | bytes 786436
  20.6 9.1 %copy-start.2 = (bf16[512,256]{1,0:T(8,128)(2,1)S(1)}, bf16[512,256]{1,0:T(8,128)(2,1)}, u32[]{:S(2)}) copy-start(bf16[512,256]{1,0:T(8,128)(2,1)} %stream_ref.5) | copy-start | bytes 786436
  20.6 9.1 %copy-start.3 = (bf16[512,256]{1,0:T(8,128)(2,1)S(1)}, bf16[512,256]{1,0:T(8,128)(2,1)}, u32[]{:S(2)}) copy-start(bf16[512,256]{1,0:T(8,128)(2,1)} %key_ref.3) | copy-start | bytes 786436
  32.5 28.0 %copy-start = (f32[1024,128]{1,0:T(8,128)S(1)}, f32[1024,128]{1,0:T(8,128)}, u32[]{:S(2)}) copy-start(f32[1024,128]{1,0:T(8,128)} %get-tuple-element.30.local_in.local_ref) | copy-start | bytes 1572868
  60.5 7.1 %copy-start.6 = (bf16[512,256]{1,0:T(8,128)(2,1)S(1)}, bf16[512,256]{1,0:T(8,128)(2,1)}, u32[]{:S(2)}) copy-start(bf16[512,256]{1,0:T(8,128)(2,1)} %grad_ref.3) | copy-start | bytes 786436
  60.5 7.2 %copy-start.9 = (bf16[1024,128]{1,0:T(8,128)(2,1)S(1)}, bf16[1024,128]{1,0:T(8,128)(2,1)}, u32[]{:S(2)}) copy-start(bf16[1024,128]{1,0:T(8,128)(2,1)} %get-tuple-element.38.signal_ref) | copy-start | bytes 786436
  60.5 7.2 %copy-start.10 = (f32[512,128]{1,0:T(8,128)S(1)}, f32[512,128]{1,0:T(8,128)}, u32[]{:S(2)}) copy-start(f32[512,128]{1,0:T(8,128)} %get-tuple-element.39.inv_ref) | copy-start | bytes 786436
  62.0 17.1 %all-to-all-start.3 = ((f32[16,4,128]{2,1,0:T(4,128)}), f32[16,4,128]{2,1,0:T(4,128)S(1)}, u32[]{:S(2)}, u32[]{:S(2)}) async-start(f32[16,4,128]{2,1,0:T(4,128)} %correct.1), calls=%async_computation.3 | async-start | bytes 65536 | tf_op jit(solution)/shard_map/all_to_all | solution.py:583
